TPU v7x, 128 devices: a whole 4x4x4 slice. The times are simulated.
128 devices in a mesh: pb: 8 (over z, core), pa: 16 (over x, y).
Axes of the slice: x: 4, y: 4, z: 4, core: 2. Of those that a mesh axis runs over, the one named last changes fastest.
Arguments:
- queries: float32 [16384, 768], P(('pb', 'pa')), may hold values from -5 to 5
- passages: float32 [16384, 768], P(('pb', 'pa')), may hold values from -5 to 5
- hard_ids: int32 [16384, 32], P(('pb', 'pa')), may hold values from 0 to 16383, as said below
- list_lengths: int32 [16384], P(('pb', 'pa')), may hold values from 1 to 32, 393216 in all
Outputs:
- loss: float32 [], replicated
- grad_queries: float32 [16384, 768], P(('pb', 'pa'))
- grad_passages: float32 [16384, 768], P(('pb', 'pa'))
Inputs may be any that keep to these rules, and one draw needn't show every extreme that they name: `hard_ids`: cut the rows into aligned blocks of 128 (the rows of one device) and the passage ids into blocks of 128 consecutive ids: the 32 listed ids of one row block, live or not, fall at most 40 times into any one id block; in every draw some id block receives exactly 40 ids from every row block.
All inputs are finite; a program needn't handle non-finite values. No bound on the sum of `list_lengths` on one device may be relied on, other than what follows from the above.
Results may differ from a plain program's by a relative error of at most 0.0014.
The roundings to bfloat16 on the way count: a program that leaves them out, or rounds other values in their place, can miss the bound.
Values may be sent and summed in bfloat16 or wider, within the bound.
A program may use at most 128 MiB of HBM per device.

v0:
```python
import functools
import math

import jax
import jax.numpy as jnp
from jax import lax
from jax.sharding import Mesh
from jax.sharding import PartitionSpec as P

PA = ("pa_0", "pa_1")
PB = ("pb_0", "pb_1")
PB_PA = ("pb_0", "pb_1", "pa_0", "pa_1")


def sent_to_all(value, axis):
    size = lax.axis_size(axis)
    return lax.all_to_all(
        jnp.broadcast_to(value[None], (size, *value.shape)), axis, 0, 0, tiled=True
    )


def in_order(blocks, dim):
    shape = list(blocks.shape[1:])
    shape[dim] *= blocks.shape[0]
    return jnp.moveaxis(blocks, 0, dim).reshape(shape)


def gather_directly(value, axis, dim):
    blocks = sent_to_all(value, axis)
    return in_order(blocks, dim)


def all_in_one(value, axis):
    leaves = jax.tree.leaves(value)
    turns = sorted(range(len(leaves)), key=lambda k: -leaves[k].size)
    width = (1, *leaves[turns[0]].shape)[-1]
    lines = [
        jnp.pad(leaves[k].reshape(-1), (0, -leaves[k].size % width)).reshape(-1, width)
        for k in turns
    ]
    both, at, found = (sent_to_all(jnp.concatenate(lines), axis), 0, {})
    for k, line in zip(turns, lines):
        share = both[:, at : at + len(line)].reshape(len(both), -1)
        found[k] = share[:, : leaves[k].size].reshape(-1, *leaves[k].shape)
        at += len(line)
    numbers = iter(range(len(leaves)))
    return jax.tree.map(lambda _: found[next(numbers)], value)


def combined_pairwise(pieces, combine):
    while len(jax.tree.leaves(pieces)[0]) > 1:
        pieces = jax.vmap(combine)(
            *(jax.tree.map(lambda part: part[side::2], pieces) for side in (0, 1))
        )
    return jax.tree.map(lambda part: part[0], pieces)


def combined_all(value, axis, combine):
    pieces = all_in_one(value, axis)
    return combined_pairwise(pieces, combine)


def by_axis(value, axes):
    return functools.reduce(lax.psum, axes, value)


def in_blocks(value, dim, size):
    before, after = (value.shape[:dim], value.shape[dim + 1 :])
    return jnp.moveaxis(value.reshape(*before, size, -1, *after), dim, 0)


def sent_and_summed(value, axis, dim):
    blocks = in_blocks(value, dim, lax.axis_size(axis))
    arrived = lax.all_to_all(blocks, axis, split_axis=0, concat_axis=0, tiled=True)
    return arrived.sum(axis=0)


def tile_scores(left_rows, right_rows):
    return lax.dot_general(
        left_rows, right_rows, (((1,), (1,)), ((), ())), preferred_element_type=jnp.float32
    )


def slot_places(owner_rank, devices):
    pair_count = owner_rank.shape[0]
    group_width = 128
    one_hot = (owner_rank[:, None] == jnp.arange(devices, dtype=jnp.int32)[None, :]).astype(
        jnp.float32
    )
    grouped = one_hot.reshape(pair_count // group_width, group_width, devices)
    lower_mask = (jnp.arange(group_width)[None, :] < jnp.arange(group_width)[:, None]).astype(
        jnp.float32
    )
    within = jnp.einsum("ij,bjd->bid", lower_mask, grouped, precision=lax.Precision.HIGHEST)
    counts = grouped.sum(1)
    before = jnp.cumsum(counts, 0) - counts
    slot_rank = jnp.sum((within + before[:, None, :]) * grouped, -1)
    return slot_rank.reshape(pair_count).astype(jnp.int32)


def combine_stats(first_pair, second_pair):
    first_top, first_total = first_pair
    second_top, second_total = second_pair
    new_top = jnp.maximum(first_top, second_top)
    return (
        new_top,
        first_total * jnp.exp(first_top - new_top) + second_total * jnp.exp(second_top - new_top),
    )


def per_device(queries, passages, hard_ids, list_lengths):
    row_count, feature_width = queries.shape
    listed = hard_ids.shape[1]
    span_across = lax.axis_size(PA)
    span_down = lax.axis_size(PB)
    devices = span_across * span_down
    capacity = (5 * listed * row_count + 4 * devices - 1) // (4 * devices)
    col_index = lax.axis_index(PA)
    row_index = lax.axis_index(PB)
    query_own = queries.astype(jnp.bfloat16)
    passage_own = passages.astype(jnp.bfloat16)
    query_block = lax.all_gather(query_own, PA, axis=0, tiled=True)
    passage_block = gather_directly(passage_own, PB, 0)
    pair_count = row_count * listed
    flat_ids = hard_ids.reshape(pair_count)
    owner_rank = flat_ids // row_count
    local_row = flat_ids % row_count
    slot_place = owner_rank * capacity + slot_places(owner_rank, devices)
    live_mask = jnp.arange(listed, dtype=jnp.int32)[None, :] < list_lengths[:, None]
    request = (
        jnp.zeros((devices * capacity,), jnp.int32)
        .at[slot_place]
        .set(local_row)
        .reshape(devices, capacity)
    )
    pair_queries = jnp.repeat(query_own, listed, axis=0)
    outgoing = (
        jnp.zeros((devices * capacity, feature_width), jnp.bfloat16)
        .at[slot_place]
        .set(pair_queries)
    )
    outgoing = outgoing.reshape(devices, capacity, feature_width)
    arrived_queries = lax.all_to_all(outgoing, PB_PA, split_axis=0, concat_axis=0, tiled=True)
    asked_rows = lax.all_to_all(request, PB_PA, split_axis=0, concat_axis=0, tiled=True)
    found_rows = passage_own[asked_rows]
    fetched = lax.all_to_all(found_rows, PB_PA, split_axis=0, concat_axis=0, tiled=True)
    neg_rows = fetched.reshape(devices * capacity, feature_width)[slot_place].reshape(
        row_count, listed, feature_width
    )
    hard_score = jnp.einsum("rd,rhd->rh", query_own, neg_rows, preferred_element_type=jnp.float32)
    masked = jnp.where(live_mask, hard_score, -jnp.inf)
    tall_rows = query_block.shape[0]
    wide_cols = passage_block.shape[0]
    block_rows = math.gcd(tall_rows, 512)

    def sweep_block(carried, query_part):
        col_top, col_total = carried
        scores = tile_scores(query_part, passage_block)
        part_top = scores.max(1)
        part_total = jnp.exp(scores - part_top[:, None]).sum(1)
        new_top = jnp.maximum(col_top, scores.max(0))
        col_total = col_total * jnp.exp(col_top - new_top) + jnp.exp(scores - new_top[None, :]).sum(
            0
        )
        return ((new_top, col_total), (part_top, part_total))

    start_state = (
        jnp.full((wide_cols,), -jnp.inf, jnp.float32),
        jnp.zeros((wide_cols,), jnp.float32),
    )
    (col_top, col_total), (row_top, row_total) = lax.scan(
        sweep_block,
        start_state,
        query_block.reshape(tall_rows // block_rows, block_rows, feature_width),
    )
    row_top = row_top.reshape(tall_rows)
    row_total = row_total.reshape(tall_rows)
    own_top = lax.dynamic_slice_in_dim(row_top, col_index * row_count, row_count)
    own_total = lax.dynamic_slice_in_dim(row_total, col_index * row_count, row_count)
    merged_top = jnp.maximum(own_top, masked.max(1))
    merged_total = own_total * jnp.exp(own_top - merged_top) + jnp.exp(
        masked - merged_top[:, None]
    ).sum(1)
    row_top = lax.dynamic_update_slice_in_dim(row_top, merged_top, col_index * row_count, 0)
    row_total = lax.dynamic_update_slice_in_dim(row_total, merged_total, col_index * row_count, 0)
    row_peak, row_sum = combined_all((row_top, row_total), PA, combine_stats)
    col_peak, col_sum = combined_all((col_top, col_total), PB, combine_stats)
    row_lse = row_peak + jnp.log(row_sum)
    column_lse = col_peak + jnp.log(col_sum)
    diagonal = jnp.einsum("rd,rd->r", query_own, passage_own, preferred_element_type=jnp.float32)
    own_row = lax.dynamic_slice_in_dim(row_lse, col_index * row_count, row_count)
    own_column = lax.dynamic_slice_in_dim(column_lse, row_index * row_count, row_count)
    partial_loss = jnp.sum(own_row - diagonal) + jnp.sum(own_column - diagonal)
    loss = by_axis(partial_loss, PB_PA) / (2.0 * row_count * devices)
    hard_weight = jnp.exp(masked - own_row[:, None]).astype(jnp.bfloat16)
    hard_query = jnp.einsum("rh,rhd->rd", hard_weight, neg_rows, preferred_element_type=jnp.float32)
    flat_weight = hard_weight.reshape(pair_count)
    slot_weight = (
        jnp.zeros((devices * capacity,), jnp.bfloat16)
        .at[slot_place]
        .set(flat_weight)
        .reshape(devices, capacity)
    )
    arrived_weight = lax.all_to_all(slot_weight, PB_PA, split_axis=0, concat_axis=0, tiled=True)
    arrived_rows = arrived_weight.astype(jnp.float32)[:, :, None] * arrived_queries.astype(
        jnp.float32
    )
    hard_passage = (
        jnp.zeros((row_count, feature_width), jnp.float32)
        .at[asked_rows.reshape(-1)]
        .add(arrived_rows.reshape(-1, feature_width))
    )
    row_span = lax.axis_size(PA) * row_count
    query_part = query_block
    level_part = row_lse
    inner_rows = math.gcd(row_span, 512)

    def query_piece_work(inputs):
        left_rows, level_rows = inputs
        scores = tile_scores(left_rows, passage_block)
        weights = (
            jnp.exp(scores - level_rows[:, None]) + jnp.exp(scores - column_lse[None, :])
        ).astype(jnp.bfloat16)
        return jnp.dot(weights, passage_block, preferred_element_type=jnp.float32)

    results = lax.map(
        query_piece_work,
        (
            query_part.reshape(row_span // inner_rows, inner_rows, feature_width),
            level_part.reshape(row_span // inner_rows, inner_rows),
        ),
    )
    query_sum = lax.psum_scatter(
        results.reshape(row_span, feature_width), PA, scatter_dimension=0, tiled=True
    )
    row_span = row_count * lax.axis_size(PB)
    level_part = column_lse
    inner_rows = math.gcd(row_span, 512)

    def passage_piece_work(inputs):
        left_rows, level_rows = inputs
        scores = tile_scores(left_rows, query_block)
        weights = (
            jnp.exp(scores - row_lse[None, :]) + jnp.exp(scores - level_rows[:, None])
        ).astype(jnp.bfloat16)
        return jnp.dot(weights, query_block, preferred_element_type=jnp.float32)

    results = lax.map(
        passage_piece_work,
        (
            passage_block.reshape(row_span // inner_rows, inner_rows, feature_width),
            level_part.reshape(row_span // inner_rows, inner_rows),
        ),
    )
    passage_sum = sent_and_summed(results.reshape(row_span, feature_width), PB, 0)
    grad_queries = 0.5 * (query_sum + hard_query - 2.0 * passage_own.astype(jnp.float32))
    grad_passages = 0.5 * (passage_sum + hard_passage - 2.0 * query_own.astype(jnp.float32))
    return (loss, grad_queries, grad_passages)


def solution(mesh):
    finer = Mesh(mesh.devices.reshape(4, 2, 4, 4), ("pb_0", "pb_1", "pa_0", "pa_1"))
    placed = (P(PB_PA, None), P(PB_PA, None), P(PB_PA, None), P(PB_PA))
    return jax.shard_map(
        per_device,
        mesh=finer,
        in_specs=placed,
        out_specs=(P(), P(PB_PA, None), P(PB_PA, None)),
        check_vma=False,
    )
```

profile of v0, /device:TPU:0, one launch (start us, length us, event | category | flops | bytes accessed | tf_op | source)
XLA Modules:
  0.0 494.4 jit_solution(18055308459338006924)
XLA Ops:
  7.2 1.8 fusion.37
  9.1 0.9 copy.10
  10.2 0.4 convert_reduce_fusion
  10.6 0.8 fusion.32
  11.6 15.5 %scatter_custom_fusion = s32[5120]{0:T(1024)S(1)} fusion(s32[4096]{0:T(1024)S(1)} %bitcast.153, s32[4096]{0:T(1024)S(1)} %add_select_fusion, s32[]{:T(128)} %copy.76), kind=kCustom, calls=%fused_computation.91 | custom fusion | bytes 20484 | tf_op jit(solution)/shard_map/scatter | solution.py:133
  27.3 20.5 %all_to_all.52 = s32[128,1,40]{2,1,0:T(1,128)S(1)} all-to-all(s32[128,1,40]{2,1,0:T(1,128)S(1)} %bitcast.148), channel_id=1, replica_groups=mesh['pb_0'=4,'pb_1'=2,'pa_0'=4,'pa_1'=4] {'pb_0','pb_1','pa_0','pa_1'}, dimensions={0} | all-to-all | bytes 40960 | tf_op jit(solution)/shard_map/all_to_all | solution.py:144
  47.8 1.3 broadcast_in_dim.41
  49.0 4.3 all-to-all-start
  53.5 21.4 %all-to-all-done = bf16[8,128,768]{2,1,0:T(8,128)(2,1)} async-done(((bf16[8,128,768]{2,1,0:T(8,128)(2,1)}), bf16[8,128,768]{2,1,0:T(8,128)(2,1)}, u32[]{:S(2)}, u32[]{:S(2)}) %all-to-all-start) | async-done | bytes 1572896 | tf_op jit(solution)/shard_map/all_to_all | solution.py:17
  74.9 14.5 %while.39 = (s32[]{:T(128)}, f32[1024]{0:T(1024)S(1)}, f32[1024]{0:T(1024)S(1)}, f32[4,512]{1,0:T(4,128)S(1)}, f32[4,512]{1,0:T(4,128)S(1)}, /*index=5*/bf16[4,5...) while((s32[]{:T(128)}, f32[1024]{0:T(1024)S(1)}, f32[1024]{0:T(1024)S(1)}, ...), condition=%wide.region_5.6_spmd.clone, body=%wide.region_0.0_spmd.clone.sunk | while | flops 808456192 | bytes 6621308 | solution.py:171
  74.9 2.7 fusion.93
  77.6 0.7 exponential_reduce_fusion.4
  78.5 2.7 fusion.93
  81.3 0.7 exponential_reduce_fusion.4
  82.1 2.8 fusion.93
  84.9 0.7 exponential_reduce_fusion.4
  85.8 2.7 fusion.93
  88.5 0.7 exponential_reduce_fusion.4
  89.4 0.6 broadcast_in_dim.44
  90.0 3.4 all-to-all-start.4
  93.4 21.9 %gather_fusion = bf16[5120,768]{1,0:T(8,128)(2,1)} fusion(bf16[128,768]{1,0:T(8,128)(2,1)S(1)} %get-tuple-element.200, s32[5120]{0:T(1024)S(1)} %broadcast_clamp_fusion), kind=kCustom, calls=%fused_computation | custom fusion | bytes 15749120 | tf_op jit(solution)/shard_map/gather | solution.py:145
  115.4 7.0 %all-to-all-start.2 = ((bf16[128,40,768]{2,1,0:T(8,128)(2,1)}), bf16[128,40,768]{2,1,0:T(8,128)(2,1)}, u32[]{:S(2)}, u32[]{:S(2)}) async-start(bf16[128,40,768]{2,1,0:T(8,128)(2,1)} %bitcast.134), calls=%async_computation.2 | async-start | bytes 15728640 | tf_op jit(solution)/shard_map/all_to_all | solution.py:146
  122.4 3.0 broadcast_in_dim.52
  125.5 23.6 %scatter_custom_fusion.2 = bf16[5120,768]{1,0:T(8,128)(2,1)} fusion(s32[4096]{0:T(1024)S(1)} %bitcast.154, bf16[4096,768]{1,0:T(8,128)(2,1)} %bitcast.138, bf16[]{:T(256)} %constant.125.clone.1), kind=kCustom, calls=%fused_computation.35 | custom fusion | bytes 7864832 | tf_op jit(solution)/shard_map/scatter | solution.py:140
  149.4 64.7 %all-to-all-done.2 = bf16[128,40,768]{2,1,0:T(8,128)(2,1)} async-done(((bf16[128,40,768]{2,1,0:T(8,128)(2,1)}), bf16[128,40,768]{2,1,0:T(8,128)(2,1)}, u32[]{:S(2)}, u32[]{:S(2)}) %all-to-all-start.2) | async-done | bytes 7864352 | tf_op jit(solution)/shard_map/all_to_all | solution.py:146
  214.1 23.3 %gather_fusion.1 = bf16[4096,768]{1,0:T(8,128)(2,1)} fusion(bf16[5120,768]{1,0:T(8,128)(2,1)} %bitcast.15, s32[4096]{0:T(1024)S(1)} %broadcast_clamp_fusion.1), kind=kCustom, calls=%fused_computation.1 | custom fusion | bytes 12599296 | tf_op jit(solution)/shard_map/gather | solution.py:147
  237.4 4.5 fusion.40
  242.5 0.8 broadcast_in_dim.43
  243.3 7.7 %all-to-all-start.3 = ((f32[16,2,2048]{2,1,0:T(2,128)}), f32[16,2,2048]{2,1,0:T(2,128)S(1)}, u32[]{:S(2)}, u32[]{:S(2)}) async-start(f32[16,2,2048]{2,1,0:T(2,128)} %broadcast_in_dim.43), calls=%async_computation.3 | async-start | bytes 524288 | tf_op jit(solution)/shard_map/all_to_all | solution.py:17
  251.1 0.5 broadcast.220
  251.6 0.7 fusion.64
  252.3 7.8 %all-to-all-done.3 = f32[16,2,2048]{2,1,0:T(2,128)S(1)} async-done(((f32[16,2,2048]{2,1,0:T(2,128)}), f32[16,2,2048]{2,1,0:T(2,128)S(1)}, u32[]{:S(2)}, u32[]{:S(2)}) %all-to-all-start.3) | async-done | bytes 262176 | tf_op jit(solution)/shard_map/all_to_all | solution.py:17
  260.1 6.8 %all-to-all-start.7 = ((bf16[128,40,768]{2,1,0:T(8,128)(2,1)}), bf16[128,40,768]{2,1,0:T(8,128)(2,1)}, u32[]{:S(2)}, u32[]{:S(2)}) async-start(bf16[128,40,768]{2,1,0:T(8,128)(2,1)} %bitcast.133), calls=%async_computation.8 | async-start | bytes 15728640 | tf_op jit(solution)/shard_map/all_to_all | solution.py:143
  266.9 0.2 fusion.67
  267.7 0.7 fusion.65
  268.4 21.1 %while.37 = (s32[]{:T(128)}, f32[4,512,768]{2,1,0:T(8,128)}, bf16[4,512,768]{2,1,0:T(8,128)(2,1)}, bf16[1024,768]{1,0:T(8,128)(2,1)}, f32[4,512]{1,0:T(4,128)S(1)}, /*index=5*/f32[1024]{0:T(1024)S(1)}, s32[]{:T(128)}) while((s32[]{:T(128)}, f32[4,512,768]{2,1,0:T(8,128)}, bf16[4,512,768]{2,1,0:T(8,128)(2,1)}, bf16[1024,768]{1,0:T(8,128)(2,1)}, ...), condition=%wide.region_19.20_spmd, body=%wide.region_18.19_spmd.sunk | while | flops 1612709888 | bytes 5516377 | solution.py:226
  268.4 5.3 %bitcast_dynamic-update-slice_fusion.4 = f32[4,512,768]{2,1,0:T(8,128)} fusion(f32[4,512,768]{2,1,0:T(8,128)} %get-tuple-element.372, s32[]{:T(128)S(6)} %copy.65, bf16[1024,768]{1,0:T(8,128)(2,1)} %get-tuple-element.381, f32[1024]{0:T(1024)S(1)} %get-tuple-element.383, f32[512]{0:T(512)S(1)} %bitcast.158, bf16[4,512,768]{2,1,0:T(8,128)(2,1)} %get-tuple-element.380), kind=kOutput, calls=%fused_computation.7.clone.1 | convolution fusion | flops 1612709888 | bytes 5512192 | tf_op jit(solution)/shard_map/while/body/eval_jaxpr/dot_general | solution.py:224
  273.7 5.3 %bitcast_dynamic-update-slice_fusion.4 = f32[4,512,768]{2,1,0:T(8,128)} fusion(f32[4,512,768]{2,1,0:T(8,128)} %get-tuple-element.372, s32[]{:T(128)S(6)} %copy.65, bf16[1024,768]{1,0:T(8,128)(2,1)} %get-tuple-element.381, f32[1024]{0:T(1024)S(1)} %get-tuple-element.383, f32[512]{0:T(512)S(1)} %bitcast.158, bf16[4,512,768]{2,1,0:T(8,128)(2,1)} %get-tuple-element.380), kind=kOutput, calls=%fused_computation.7.clone.1 | convolution fusion | flops 1612709888 | bytes 5512192 | tf_op jit(solution)/shard_map/while/body/eval_jaxpr/dot_general | solution.py:224
  279.0 5.2 %bitcast_dynamic-update-slice_fusion.4 = f32[4,512,768]{2,1,0:T(8,128)} fusion(f32[4,512,768]{2,1,0:T(8,128)} %get-tuple-element.372, s32[]{:T(128)S(6)} %copy.65, bf16[1024,768]{1,0:T(8,128)(2,1)} %get-tuple-element.381, f32[1024]{0:T(1024)S(1)} %get-tuple-element.383, f32[512]{0:T(512)S(1)} %bitcast.158, bf16[4,512,768]{2,1,0:T(8,128)(2,1)} %get-tuple-element.380), kind=kOutput, calls=%fused_computation.7.clone.1 | convolution fusion | flops 1612709888 | bytes 5512192 | tf_op jit(solution)/shard_map/while/body/eval_jaxpr/dot_general | solution.py:224
  284.2 5.2 %bitcast_dynamic-update-slice_fusion.4 = f32[4,512,768]{2,1,0:T(8,128)} fusion(f32[4,512,768]{2,1,0:T(8,128)} %get-tuple-element.372, s32[]{:T(128)S(6)} %copy.65, bf16[1024,768]{1,0:T(8,128)(2,1)} %get-tuple-element.381, f32[1024]{0:T(1024)S(1)} %get-tuple-element.383, f32[512]{0:T(512)S(1)} %bitcast.158, bf16[4,512,768]{2,1,0:T(8,128)(2,1)} %get-tuple-element.380), kind=kOutput, calls=%fused_computation.7.clone.1 | convolution fusion | flops 1612709888 | bytes 5512192 | tf_op jit(solution)/shard_map/while/body/eval_jaxpr/dot_general | solution.py:224
  289.5 0.5 broadcast.222
  290.0 0.8 reduce.13
  290.9 0.7 fusion.62
  292.8 0.7 reshape.338
  293.5 21.8 %psum.28 = f32[]{:T(128)} all-reduce(f32[]{:T(128)S(6)} %add.197), channel_id=1, replica_groups=mesh['pb_0'=4,'pb_1'=2,'pa_0'=4,'pa_1'=4] {'pb_0'}, use_global_device_ids=true, to_apply=%region_14.15 | all-reduce | flops 1 | bytes 8 | tf_op jit(solution)/shard_map/psum | solution.py:64
  315.3 3.3 psum.29
  318.7 28.6 %scatter_custom_fusion.1 = bf16[5120]{0:T(1024)(128)(2,1)S(1)} fusion(s32[4096]{0:T(1024)S(1)} %bitcast.156, bf16[4096]{0:T(1024)(128)(2,1)S(1)} %reshape.372, bf16[]{:T(256)} %constant.125.clone.1), kind=kCustom, calls=%fused_computation.102 | custom fusion | bytes 10242 | tf_op jit(solution)/shard_map/scatter | solution.py:201
  347.3 0.8 all_to_all.43
  348.1 19.4 %all-to-all-done.7 = bf16[128,40,768]{2,1,0:T(8,128)(2,1)} async-done(((bf16[128,40,768]{2,1,0:T(8,128)(2,1)}), bf16[128,40,768]{2,1,0:T(8,128)(2,1)}, u32[]{:S(2)}, u32[]{:S(2)}) %all-to-all-start.7) | async-done | bytes 7864352 | tf_op jit(solution)/shard_map/all_to_all | solution.py:143
  367.5 13.7 %all-to-all-start.6 = ((bf16[128,1,40]{2,1,0:T(2,128)(2,1)}), bf16[128,1,40]{2,1,0:T(2,128)(2,1)S(1)}, u32[]{:S(2)}, u32[]{:S(2)}) async-start(bf16[128,1,40]{2,1,0:T(2,128)(2,1)} %all_to_all.43), calls=%async_computation.7 | async-start | bytes 131072 | tf_op jit(solution)/shard_map/all_to_all | solution.py:204
  381.2 13.9 %while.38 = (s32[]{:T(128)}, f32[2,512,768]{2,1,0:T(8,128)S(1)}, bf16[2,512,768]{2,1,0:T(8,128)(2,1)}, bf16[2048,768]{1,0:T(8,128)(2,1)}, f32[2048]{0:T(1024)S(1)}, /*index=5*/f32[2,512]{1,0:T(2,128)S(1)}, s32[]{:T(128)}) while((s32[]{:T(128)}, f32[2,512,768]{2,1,0:T(8,128)S(1)}, bf16[2,512,768]{2,1,0:T(8,128)(2,1)}, ...), condition=%wide.region_22.23_spmd, body=%wide.region_21.22_spmd.sunk | while | flops 3225419776 | bytes 8666201 | solution.py:248
  381.2 7.0 %bitcast_dynamic-update-slice_fusion.5 = f32[2,512,768]{2,1,0:T(8,128)S(1)} fusion(f32[2,512,768]{2,1,0:T(8,128)S(1)} %get-tuple-element.393, s32[]{:T(128)S(6)} %copy.71, bf16[2048,768]{1,0:T(8,128)(2,1)} %get-tuple-element.402, f32[512]{0:T(512)S(1)} %bitcast.159, f32[2048]{0:T(1024)S(1)} %get-tuple-element.403, ...), kind=kOutput, calls=%fused_computation.19.clone.1 | convolution fusion | flops 3225419776 | bytes 8662016 | tf_op jit(solution)/shard_map/while/body/eval_jaxpr/dot_general | solution.py:246
  388.3 6.8 %bitcast_dynamic-update-slice_fusion.5 = f32[2,512,768]{2,1,0:T(8,128)S(1)} fusion(f32[2,512,768]{2,1,0:T(8,128)S(1)} %get-tuple-element.393, s32[]{:T(128)S(6)} %copy.71, bf16[2048,768]{1,0:T(8,128)(2,1)} %get-tuple-element.402, f32[512]{0:T(512)S(1)} %bitcast.159, f32[2048]{0:T(1024)S(1)} %get-tuple-element.403, ...), kind=kOutput, calls=%fused_computation.19.clone.1 | convolution fusion | flops 3225419776 | bytes 8662016 | tf_op jit(solution)/shard_map/while/body/eval_jaxpr/dot_general | solution.py:246
  395.1 10.3 %psum.30 = f32[]{:T(128)} all-reduce(f32[]{:T(128)} %psum.29), channel_id=1, replica_groups=mesh['pb_0'=4,'pb_1'=2,'pa_0'=4,'pa_1'=4] {'pa_0'}, use_global_device_ids=true, to_apply=%region_16.17 | all-reduce | flops 1 | bytes 8 | tf_op jit(solution)/shard_map/psum | solution.py:64
  405.4 0.6 copy-done.8
  406.0 4.7 all-to-all-start.5
  410.7 0.6 compare_select_fusion.1
  411.3 11.1 %psum.31 = f32[]{:T(128)} all-reduce(f32[]{:T(128)} %psum.30), channel_id=1, replica_groups=mesh['pb_0'=4,'pb_1'=2,'pa_0'=4,'pa_1'=4] {'pa_1'}, use_global_device_ids=true, to_apply=%region_17.18 | all-reduce | flops 1 | bytes 8 | tf_op jit(solution)/shard_map/psum | solution.py:64
  423.2 4.5 fusion.42
  427.7 10.0 %convert_multiply_fusion = f32[128,40,768]{2,1,0:T(8,128)} fusion(bf16[128,40,768]{2,1,0:T(8,128)(2,1)} %all-to-all-done.7, f32[128,40]{1,0:T(8,128)S(1)} %bitcast.147), kind=kLoop, calls=%fused_computation.34 | loop fusion | flops 7864320 | bytes 23613440 | tf_op jit(solution)/shard_map/mul | solution.py:205
  437.7 11.4 %all-to-all-done.5 = f32[8,128,768]{2,1,0:T(8,128)S(1)} async-done(((f32[8,128,768]{2,1,0:T(8,128)}), f32[8,128,768]{2,1,0:T(8,128)S(1)}, u32[]{:S(2)}, u32[]{:S(2)}) %all-to-all-start.5) | async-done | bytes 3145760 | tf_op jit(solution)/shard_map/all_to_all | solution.py:74
  449.3 34.5 %scatter_fusion = f32[128,768]{1,0:T(8,128)S(1)} fusion(f32[128,768]{1,0:T(8,128)S(1)} %reduce_sum.77, s32[5120]{0:T(1024)} %bitcast.152, f32[5120,768]{1,0:T(8,128)} %bitcast.132), kind=kCustom, calls=%fused_computation.5 | custom fusion | flops 3932160 | bytes 47206400 | tf_op jit(solution)/shard_map/scatter-add | solution.py:211
  483.8 0.8 fusion.39
  484.6 1.8 fusion.36
  (122 shorter events, 3.4 us)
Async XLA Ops:
  7.2 67.7 %all-gather.2.cloned.1.call-start = ((), (), s32[]{:S(2)}) async-start(), calls=%async_computation.9 | async-start | bytes 3342336 | tf_op jit(solution)/shard_map/all_gather | solution.py:122
  9.0 84.4 %copy-start = (bf16[128,768]{1,0:T(8,128)(2,1)}, bf16[128,768]{1,0:T(8,128)(2,1)S(1)}, u32[]{:S(2)}) copy-start(bf16[128,768]{1,0:T(8,128)(2,1)S(1)} %get-tuple-element.200) | copy-start | bytes 589828
  49.0 25.9 %all-to-all-start = ((bf16[8,128,768]{2,1,0:T(8,128)(2,1)}), bf16[8,128,768]{2,1,0:T(8,128)(2,1)}, u32[]{:S(2)}, u32[]{:S(2)}) async-start(bf16[8,128,768]{2,1,0:T(8,128)(2,1)} %broadcast_in_dim.41), calls=%async_computation | async-start | bytes 3145728 | tf_op jit(solution)/shard_map/all_to_all | solution.py:17
  90.0 25.3 %all-to-all-start.4 = ((f32[8,2,1024]{2,1,0:T(2,128)}), f32[8,2,1024]{2,1,0:T(2,128)S(1)}, u32[]{:S(2)}, u32[]{:S(2)}) async-start(f32[8,2,1024]{2,1,0:T(2,128)} %broadcast_in_dim.44), calls=%async_computation.4 | async-start | bytes 131072 | tf_op jit(solution)/shard_map/all_to_all | solution.py:17
  115.4 7.0 %copy-start.2 = (bf16[128,768]{1,0:T(8,128)(2,1)S(1)}, bf16[128,768]{1,0:T(8,128)(2,1)}, u32[]{:S(2)}) copy-start(bf16[128,768]{1,0:T(8,128)(2,1)} %get-tuple-element.199) | copy-start | bytes 589828
  115.4 98.7 %all-to-all-start.2 = ((bf16[128,40,768]{2,1,0:T(8,128)(2,1)}), bf16[128,40,768]{2,1,0:T(8,128)(2,1)}, u32[]{:S(2)}, u32[]{:S(2)}) async-start(bf16[128,40,768]{2,1,0:T(8,128)(2,1)} %bitcast.134), calls=%async_computation.2 | async-start | bytes 15728640 | tf_op jit(solution)/shard_map/all_to_all | solution.py:146
  237.4 4.5 copy-start.11
  241.9 76.6 %copy-start.6 = (f32[128,1,32]{2,1,0:T(1,128)}, f32[128,1,32]{2,1,0:T(1,128)S(1)}, u32[]{:S(2)}) copy-start(f32[128,1,32]{2,1,0:T(1,128)S(1)} %fusion.40) | copy-start | bytes 49156
  243.3 16.8 %all-to-all-start.3 = ((f32[16,2,2048]{2,1,0:T(2,128)}), f32[16,2,2048]{2,1,0:T(2,128)S(1)}, u32[]{:S(2)}, u32[]{:S(2)}) async-start(f32[16,2,2048]{2,1,0:T(2,128)} %broadcast_in_dim.43), calls=%async_computation.3 | async-start | bytes 524288 | tf_op jit(solution)/shard_map/all_to_all | solution.py:17
  260.1 107.4 %all-to-all-start.7 = ((bf16[128,40,768]{2,1,0:T(8,128)(2,1)}), bf16[128,40,768]{2,1,0:T(8,128)(2,1)}, u32[]{:S(2)}, u32[]{:S(2)}) async-start(bf16[128,40,768]{2,1,0:T(8,128)(2,1)} %bitcast.133), calls=%async_computation.8 | async-start | bytes 15728640 | tf_op jit(solution)/shard_map/all_to_all | solution.py:143
  266.9 217.7 %reduce-scatter.2.cloned.1.call-start = ((), (), s32[]{:S(2)}) async-start(), calls=%async_computation.10 | async-start | bytes 6684672 | tf_op jit(solution)/shard_map/reduce_scatter | solution.py:233
  367.5 37.9 %all-to-all-start.6 = ((bf16[128,1,40]{2,1,0:T(2,128)(2,1)}), bf16[128,1,40]{2,1,0:T(2,128)(2,1)S(1)}, u32[]{:S(2)}, u32[]{:S(2)}) async-start(bf16[128,1,40]{2,1,0:T(2,128)(2,1)} %all_to_all.43), calls=%async_computation.7 | async-start | bytes 131072 | tf_op jit(solution)/shard_map/all_to_all | solution.py:204
  395.1 10.3 %copy-start.4 = (f32[2,512,768]{2,1,0:T(8,128)}, f32[2,512,768]{2,1,0:T(8,128)S(1)}, u32[]{:S(2)}) copy-start(f32[2,512,768]{2,1,0:T(8,128)S(1)} %get-tuple-element.112) | copy-start | bytes 9437188
  405.4 0.6 copy-start.8
  405.4 5.3 %copy-start.10 = (s32[5120,1]{0,1:T(1,128)S(1)}, s32[5120,1]{0,1:T(1,128)}, u32[]{:S(2)}) copy-start(s32[5120,1]{0,1:T(1,128)} %reshape.338) | copy-start | bytes 61444
  405.4 17.6 %copy-start.7 = (f32[128,1,32]{2,1,0:T(1,128)S(1)}, f32[128,1,32]{2,1,0:T(1,128)}, u32[]{:S(2)}) copy-start(f32[128,1,32]{2,1,0:T(1,128)} %copy-done.6) | copy-start | bytes 49156
  406.0 43.1 %all-to-all-start.5 = ((f32[8,128,768]{2,1,0:T(8,128)}), f32[8,128,768]{2,1,0:T(8,128)S(1)}, u32[]{:S(2)}, u32[]{:S(2)}) async-start(f32[8,128,768]{2,1,0:T(8,128)} %bitcast.140), calls=%async_computation.6 | async-start | bytes 6291456 | tf_op jit(solution)/shard_map/all_to_all | solution.py:74
  423.2 4.5 copy-start.9
  449.3 34.5 %copy-start.3 = (bf16[128,768]{1,0:T(8,128)(2,1)S(1)}, bf16[128,768]{1,0:T(8,128)(2,1)}, u32[]{:S(2)}) copy-start(bf16[128,768]{1,0:T(8,128)(2,1)} %get-tuple-element.199) | copy-start | bytes 589828
  449.3 35.3 %copy-start.1 = (bf16[128,768]{1,0:T(8,128)(2,1)S(1)}, bf16[128,768]{1,0:T(8,128)(2,1)}, u32[]{:S(2)}) copy-start(bf16[128,768]{1,0:T(8,128)(2,1)} %copy-done) | copy-start | bytes 589828
  449.3 35.3 %copy-start.5 = (f32[128,1,768]{2,1,0:T(1,128)S(1)}, f32[128,1,768]{2,1,0:T(1,128)}, u32[]{:S(2)}) copy-start(f32[128,1,768]{2,1,0:T(1,128)} %fusion.42) | copy-start | bytes 1179652
Sparse Core Ops, SparseCore 0:
  10.2 50.1 all-gather.1
  289.6 127.9 reduce-scatter.1
where the time goes:
time: 496 us; the launch traced here: 494 us
  local copies, waits for them, and re-layouts  125 us (25%)
  waiting for transfers between devices  125 us (25%)
  blocking collectives  66.9 us (13%)
  other arithmetic  57 us (11%)
  matrix products  55.7 us (11%)
  starting transfers between devices  47.6 us (10%)
  between operations  17.6 us (4%)
    all_to_all x1, waiting for transfers between devices, per_device(): lax.all_to_all(found_rows, PB_PA, split_axis=0, concat_axis=0, tiled=True)  64.7 us
    psum x4, blocking collectives, by_axis(): return functools.reduce(lax.psum, axes, value)  46.4 us
    scatter-add x1, other arithmetic, per_device(): hard_passage = jnp.zeros((row_count, feature_width), jnp.float32).at[aske...  34.5 us
    all_to_all x3, waiting for transfers between devices, sent_to_all(): lax.all_to_all(jnp.broadcast_to(value[None], (size, *value.shape)), axis,...  29.3 us
    scatter x1, local copies, waits for them, and re-layouts, per_device(): slot_weight = jnp.zeros((devices * capacity,), jnp.bfloat16).at[slot_plac...  28.6 us
    scatter x1, local copies, waits for them, and re-layouts, per_device(): outgoing = jnp.zeros((devices * capacity, feature_width), jnp.bfloat16).a...  23.6 us
    gather x1, local copies, waits for them, and re-layouts, per_device(): fetched.reshape(devices * capacity, feature_width)[slot_place]  23.3 us
    gather x1, local copies, waits for them, and re-layouts, per_device(): found_rows = passage_own[asked_rows]  21.9 us
  transfers between devices with their start and end apart: 9, of which 5 were waited for; matrix products, arithmetic and copies ran while one was open for 38% of the time, Pallas kernels for 0%

commit v1 on v0

v1 whole, which is shorter than its diff:
```python
import functools

import jax
import jax.numpy as jnp
from jax import lax
from jax.experimental import pallas as pl
from jax.experimental.pallas import tpu as pltpu
from jax.sharding import PartitionSpec as P

BF = jnp.bfloat16
F32 = jnp.float32
MESH = pl.DeviceIdType.MESH
D = 768
OWN = 128
NQ = 8
NP = 8
QB = 256
COLS = 1024
ROWS = 2048
CH = 32
NEG = float("-inf")


def dot_nt(a, b):
    return lax.dot_general(a, b, (((1,), (1,)), ((), ())), preferred_element_type=F32)


def dot_nn(a, b):
    return lax.dot_general(a, b, (((1,), (0,)), ((), ())), preferred_element_type=F32)


def dot_tn(a, b):
    return lax.dot_general(a, b, (((0,), (0,)), ((), ())), preferred_element_type=F32)


def eighths(value):
    return value.reshape(value.shape[0] // 8, 8, value.shape[1])


def kernel(
    q_ref,
    p_ref,
    dest_ref,
    code_ref,
    loss_ref,
    gq_ref,
    gp_ref,
    qbuf,
    pbuf,
    sbuf,
    mbuf,
    wbuf,
    table,
    tabs,
    cmax,
    csum,
    stat,
    rstat,
    cstat,
    lrow,
    lcol,
    loss_r,
    loss_c,
    dq,
    sib,
    outq,
    inq,
    dp,
    outp,
    inp,
    q_send,
    q_recv,
    p_send,
    p_recv,
    sib_send,
    sib_recv,
    tab_send,
    tab_recv,
    rs_send,
    rs_recv,
    cs_send,
    cs_recv,
    lr_send,
    lr_recv,
    lc_send,
    lc_recv,
    dsib_send,
    dsib_recv,
    gq_send,
    gq_recv,
    gp_send,
    gp_recv,
):
    pb = lax.axis_index("pb")
    pa = lax.axis_index("pa")
    z, h = pb // 2, pb % 2
    x, y = pa // 4, pa % 4
    pair = z // 2
    zs = z % 2
    zc = (z + 3) % 4
    half, sel = zc // 2, zc % 2
    me_q = x * 2 + zs
    me_p = sel * 4 + y
    me_row = me_q * 2 + h

    def device(xx, yy, zz, hh):
        return (zz * 2 + hh, xx * 4 + yy)

    def row_peer(idx):
        q, hh = idx // 2, idx % 2
        return device(q // 2, y, pair * 2 + q % 2, hh)

    def col_peer(p):
        return device(x, p % 4, (half * 2 + p // 4 + 1) % 4, h)

    def chip_peer(q):
        return device(q // 2, y, pair * 2 + q % 2, h)

    sibling = device(x, y, z, 1 - h)

    def remote(src, dst, send, recv, to):
        return pltpu.make_async_remote_copy(
            src_ref=src,
            dst_ref=dst,
            send_sem=send,
            recv_sem=recv,
            device_id=to,
            device_id_type=MESH,
        )

    barrier = pltpu.get_barrier_semaphore()

    def greet_row(j, carry):
        pl.semaphore_signal(
            barrier, inc=1, device_id=row_peer((me_row + j) % 16), device_id_type=MESH
        )
        return carry

    def greet_col(j, carry):
        pl.semaphore_signal(
            barrier, inc=1, device_id=col_peer((me_p + j) % 8), device_id_type=MESH
        )
        return carry

    lax.fori_loop(1, 16, greet_row, 0)
    lax.fori_loop(1, 8, greet_col, 0)
    pl.semaphore_wait(barrier, 22)

    def q_at(xx, zz, first=0, size=OWN):
        return qbuf.at[xx * 2 + zz, pl.ds(pl.multiple_of(h * OWN + first, 64), size), :]

    def p_at(yy, ss, first=0, size=OWN):
        return pbuf.at[ss * 4 + yy, pl.ds(first, size), :]

    def ring(at, pos, side, to_left, to_right, to_pair, send, recv):
        left, right, far = (pos + 3) % 4, (pos + 1) % 4, (pos + 2) % 4
        other = 1 - side

        def own(src):
            here = at(pos, side)
            return [
                remote(src, here, send.at[0], recv.at[0], to_right),
                remote(src, here, send.at[1], recv.at[1], to_left),
                remote(src, here, send.at[2], recv.at[2], to_pair),
            ]

        def passing(ref, k, to):
            return remote(ref, ref, send.at[k], recv.at[k], to)

        forwards = [
            passing(at(left, side, 0, 64), 3, to_right),
            passing(at(right, side, 64, 64), 4, to_left),
            passing(at(pos, other), 5, to_right),
            passing(at(pos, other), 6, to_left),
            passing(at(far, side), 7, to_pair),
        ]
        arriving = [
            at(left, side),
            at(right, side),
            at(pos, other),
            at(far, side, 0, 64),
            at(far, side, 64, 64),
            at(left, other),
            at(right, other),
            at(far, other),
        ]
        waits = [
            remote(ref, ref, send.at[k], recv.at[k], to_pair) for k, ref in enumerate(arriving)
        ]
        return own, forwards, waits

    q_own, q_fwd, q_wait = ring(
        q_at,
        x,
        zs,
        device((x + 3) % 4, y, z, h),
        device((x + 1) % 4, y, z, h),
        device(x, y, pair * 2 + 1 - zs, h),
        q_send,
        q_recv,
    )
    p_own, p_fwd, p_wait = ring(
        p_at,
        y,
        sel,
        device(x, (y + 3) % 4, z, h),
        device(x, (y + 1) % 4, z, h),
        device(x, y, (half * 2 + (1 - sel) + 1) % 4, h),
        p_send,
        p_recv,
    )
    q_sends = q_own(q_ref)
    p_sends = p_own(p_ref)
    for one, two in zip(q_sends, p_sends):
        one.start()
        two.start()

    kinds = [
        (x, zs),
        ((x + 3) % 4, zs),
        ((x + 1) % 4, zs),
        (x, 1 - zs),
        ((x + 2) % 4, zs),
        ((x + 3) % 4, 1 - zs),
        ((x + 1) % 4, 1 - zs),
        ((x + 2) % 4, 1 - zs),
    ]

    def to_sibling(k, src=None):
        ref = q_at(*kinds[k])
        return remote(ref if src is None else src, ref, sib_send.at[k], sib_recv.at[k], sibling)

    def from_sibling(k):
        xx, zz = kinds[k]
        ref = qbuf.at[xx * 2 + zz, pl.ds(pl.multiple_of((1 - h) * OWN, OWN), OWN), :]
        return remote(ref, ref, sib_send.at[k], sib_recv.at[k], sibling)

    sib_copies = [to_sibling(k, q_ref if k == 0 else None) for k in range(8)]
    sib_copies[0].start()
    qbuf[me_q, pl.ds(pl.multiple_of(h * OWN, OWN), OWN), :] = q_ref[...]
    pbuf[me_p] = p_ref[...]

    sub = lax.broadcasted_iota(jnp.int32, (128, 128), 0)
    lane = lax.broadcasted_iota(jnp.int32, (128, 128), 1)
    earlier = jnp.where(sub < lane, 1.0, 0.0).astype(BF)
    prefix = jnp.concatenate([earlier, jnp.ones((128, 128), BF)], axis=1)
    row_code = (lane + 1 + 128 * h).astype(F32)
    offset = (64 * h).astype(F32)
    sub_f = sub.astype(F32)
    table[...] = jnp.zeros_like(table)

    def slot_step(k, count):
        dest = dest_ref[pl.ds(k, 1), :]
        code = code_ref[pl.ds(k, 1), :]
        live = jnp.where(sub == dest, 1.0, 0.0)
        both = dot_nn(live.astype(BF), prefix)
        rank = jnp.sum(live * (both[:, :128] + count), axis=0, keepdims=True) + offset
        slot = sub_f == rank
        chosen = jnp.concatenate(
            [jnp.where(slot, row_code, 0.0), jnp.where(slot, code, 0.0)], axis=0
        ).astype(BF)
        table[...] += dot_nt(live.astype(BF), chosen)
        return count + both[:, 128:]

    lax.fori_loop(0, 32, slot_step, jnp.zeros((128, 128), F32), unroll=2)

    for k in range(3):
        q_wait[k].wait_recv()
        if k < 2:
            q_fwd[k].start()
        else:
            q_fwd[2].start()
            q_fwd[3].start()
        p_wait[k].wait_recv()
        if k < 2:
            p_fwd[k].start()
        else:
            p_fwd[2].start()
            p_fwd[3].start()
        sib_copies[k + 1].start()

    def tab_copy(idx, to):
        q, hh = to // 2, to % 2
        zz = (pair * 2 + q % 2 + 3) % 4
        group = (q // 2) * 4 + (zz // 2) * 2 + hh
        return remote(
            table.at[pl.ds(pl.multiple_of(group * 8, 8), 8), :],
            tabs.at[idx],
            tab_send.at[to],
            tab_recv.at[idx],
            row_peer(to),
        )

    def tab_start(j, carry):
        tab_copy(me_row, (me_row + j) % 16).start()
        return carry

    lax.fori_loop(1, 16, tab_start, 0)
    tabs[me_row] = table[pl.ds(pl.multiple_of((x * 4 + half * 2 + h) * 8, 8), 8), :]

    for k in (3, 4):
        q_wait[k].wait_recv()
        p_wait[k].wait_recv()
    q_fwd[4].start()
    p_fwd[4].start()
    sib_copies[4].start()

    def tab_arrive(j, carry):
        other = (me_row + j) % 16
        ref = tabs.at[other]
        remote(ref, ref, tab_send.at[other], tab_recv.at[other], row_peer(other)).wait_recv()
        return carry

    lax.fori_loop(1, 16, tab_arrive, 0)

    tall = (lax.broadcasted_iota(jnp.int32, (QB, 128), 0) + 1).astype(F32)

    def count_step(q, carry):
        both = tabs[2 * q] + tabs[2 * q + 1]
        for p in range(NP):
            rows = jnp.where(tall == both[p : p + 1, :128], 1.0, 0.0).astype(BF)
            cols = jnp.where(tall[:128] == both[p : p + 1, 128:], 1.0, 0.0).astype(BF)
            mbuf[q, :, p * 128 : (p + 1) * 128] = dot_nt(rows, cols).astype(BF)
        return carry

    lax.fori_loop(0, NQ, count_step, 0)

    for k in (5, 6, 7):
        q_wait[k].wait_recv()
        sib_copies[k].start()
        p_wait[k].wait_recv()
    for k in range(8):
        from_sibling(k).wait_recv()

    cmax[...] = jnp.full(cmax.shape, NEG, F32)
    csum[...] = jnp.zeros_like(csum)
    first_half = lax.broadcasted_iota(jnp.int32, (CH, 128), 1) < 64

    def sweep(q, carry):
        for c in range(4):
            cols = slice(c * 256, (c + 1) * 256)
            part = dot_nt(qbuf[q], pbuf[2 * c : 2 * c + 2].reshape(256, D))
            sbuf[q, :, cols] = part
            old = cmax[:, cols]
            new = jnp.maximum(old, eighths(part).max(0))
            csum[:, cols] = csum[:, cols] * jnp.exp(old - new)
            cmax[:, cols] = new

        def chunk(r, inner):
            rows = pl.ds(pl.multiple_of(r * CH, CH), CH)
            top = sbuf[q, rows, 0:128]
            for g in range(1, 8):
                top = jnp.maximum(top, sbuf[q, rows, g * 128 : (g + 1) * 128])
            top = jnp.max(top, axis=1, keepdims=True)
            wide = jnp.broadcast_to(top, (CH, 128))
            total = jnp.zeros((CH, 128), F32)
            for g in range(8):
                cols = slice(g * 128, (g + 1) * 128)
                s = sbuf[q, rows, cols]
                e = jnp.exp(s - wide)
                total += e + e * mbuf[q, rows, cols].astype(F32)
                csum[:, cols] += jnp.exp(eighths(s) - cmax[:, cols][None]).sum(0)
            total = jnp.sum(total, axis=1, keepdims=True)
            stat[rows, :] = jnp.where(first_half, wide, total)
            return inner

        lax.fori_loop(0, QB // CH, chunk, 0)
        turned = stat[...].T
        rstat[me_row, pl.ds(q, 1), :] = turned[0:1, :]
        rstat[me_row, pl.ds(8 + q, 1), :] = turned[64:65, :]
        return carry

    lax.fori_loop(0, NQ, sweep, 0)

    top = jnp.max(cmax[...], axis=0, keepdims=True)
    cstat[me_p, 0:1, :] = top
    cstat[me_p, 1:2, :] = jnp.sum(csum[...] * jnp.exp(cmax[...] - top), axis=0, keepdims=True)
    diag = eighths(q_ref[...].astype(F32) * p_ref[...].astype(F32)).sum(0)
    diag = diag[:, :256] + diag[:, 256:512] + diag[:, 512:]
    rstat[me_row, 16:24, :] = diag

    def all_row(buf, send, recv):
        def start(j, carry):
            to = (me_row + j) % 16
            here = buf.at[me_row]
            remote(here, here, send.at[to], recv.at[me_row], row_peer(to)).start()
            return carry

        def arrive(j, carry):
            other = (me_row + j) % 16
            ref = buf.at[other]
            remote(ref, ref, send.at[other], recv.at[other], row_peer(other)).wait_recv()
            return carry

        return start, arrive

    def all_col(buf, send, recv):
        def start(j, carry):
            to = (me_p + j) % 8
            here = buf.at[me_p]
            remote(here, here, send.at[to], recv.at[me_p], col_peer(to)).start()
            return carry

        def arrive(j, carry):
            other = (me_p + j) % 8
            ref = buf.at[other]
            remote(ref, ref, send.at[other], recv.at[other], col_peer(other)).wait_recv()
            return carry

        return start, arrive

    rs_start, rs_arrive = all_row(rstat, rs_send, rs_recv)
    cs_start, cs_arrive = all_col(cstat, cs_send, cs_recv)
    lax.fori_loop(1, 8, cs_start, 0)
    lax.fori_loop(1, 16, rs_start, 0)
    lax.fori_loop(1, 8, cs_arrive, 0)

    tops = [cstat[k, 0:1, :] for k in range(8)]
    peak = functools.reduce(jnp.maximum, tops)
    total = functools.reduce(
        jnp.add, [cstat[k, 1:2, :] * jnp.exp(tops[k] - peak) for k in range(8)]
    )
    column_lse = peak + jnp.log(total)
    lcol[...] = jnp.broadcast_to(column_lse, (8, COLS))

    lax.fori_loop(1, 16, rs_arrive, 0)
    peak = rstat[0, 0:8, :]
    for k in range(1, 16):
        peak = jnp.maximum(peak, rstat[k, 0:8, :])
    total = jnp.zeros((8, QB), F32)
    diag = jnp.zeros((8, QB), F32)
    for k in range(16):
        total += rstat[k, 8:16, :] * jnp.exp(rstat[k, 0:8, :] - peak)
        diag += rstat[k, 16:24, :]
    row_lse = peak + jnp.log(total)
    for q in range(NQ):
        lrow[q] = jnp.broadcast_to(row_lse[q : q + 1, :], (128, QB)).T
    part = row_lse - 2.0 * diag
    loss_r[me_p] = part[:, :128] + part[:, 128:]
    part = functools.reduce(jnp.add, [column_lse[:, g * 128 : (g + 1) * 128] for g in range(8)])
    loss_c[me_row] = jnp.where(sub[:8] == 0, jnp.broadcast_to(part, (8, 128)), 0.0)

    def to_own(q):
        low = pl.multiple_of(h * OWN, OWN)
        high = pl.multiple_of((1 - h) * OWN, OWN)
        return dq.at[q, pl.ds(low, OWN), :], dq.at[q, pl.ds(high, OWN), :]

    def dsib_copy(q):
        return remote(to_own(q)[1], sib.at[q], dsib_send.at[q], dsib_recv.at[q], sibling)

    def gq_copy(q):
        return remote(outq.at[q], inq.at[me_q], gq_send.at[q], gq_recv.at[me_q], chip_peer(q))

    def gp_copy(p):
        return remote(outp.at[p], inp.at[me_p], gp_send.at[p], gp_recv.at[me_p], col_peer(p))

    def turn_q(i):
        return (me_q + 1 + i) % NQ

    def weights(q):
        def chunk(r, inner):
            rows = pl.ds(pl.multiple_of(r * CH, CH), CH)
            level = lrow[q, rows, :]
            for g in range(8):
                cols = slice(g * 128, (g + 1) * 128)
                s = sbuf[q, rows, cols]
                er = jnp.exp(s - level)
                ec = jnp.exp(eighths(s) - lcol[:, cols][None]).reshape(CH, 128)
                pair_weight = (er + ec).astype(BF).astype(F32)
                hard_weight = er.astype(BF).astype(F32)
                count = mbuf[q, rows, cols].astype(F32)
                wbuf[q, rows, cols] = (pair_weight + count * hard_weight).astype(BF)
            return inner

        lax.fori_loop(0, QB // CH, chunk, 0)

    def query_sum(q):
        everything = pbuf[...].reshape(COLS, D)
        for n in range(3):
            cols = slice(n * 256, (n + 1) * 256)
            dq[q, :, cols] = dot_nn(wbuf[q], everything[:, cols])

    def take_sibling(q):
        dsib_copy(q).wait_recv()
        low = pl.multiple_of(h * OWN, OWN)
        outq[q] = (dq[q, pl.ds(low, OWN), :] + sib[q]).astype(BF)

    def second(i, carry):
        q = turn_q(i)
        weights(q)

        @pl.when(i > 0)
        def _():
            dsib_copy(turn_q(i - 1)).start()

        @pl.when(i > 1)
        def _():
            gq_copy(turn_q(i - 2)).start()

        query_sum(q)

        @pl.when(i > 0)
        def _():
            take_sibling(turn_q(i - 1))

        return carry

    lax.fori_loop(0, NQ, second, 0)

    def turn_p(i):
        return (me_p // 2 + 1 + i) % 4

    def send_pair(i):
        for k in range(2):
            p = turn_p(i) * 2 + k

            @pl.when(p != me_p)
            def _():
                gp_copy(p).start()

    lr_start, lr_arrive = all_col(loss_r, lr_send, lr_recv)
    lc_start, lc_arrive = all_row(loss_c, lc_send, lc_recv)

    def third(i, carry):
        block = turn_p(i)
        cols = pl.ds(pl.multiple_of(block * 256, 256), 256)
        left = wbuf[:, :, cols].reshape(ROWS, 256)
        part = dot_tn(left, qbuf[...].reshape(ROWS, D))
        dp[...] = part.reshape(2, OWN, D)
        for k in range(2):
            outp[block * 2 + k] = part[k * OWN : (k + 1) * OWN].astype(BF)

        @pl.when(i == 0)
        def _():
            dsib_copy(turn_q(NQ - 1)).start()
            gq_copy(turn_q(NQ - 2)).start()
            lax.fori_loop(1, 8, lr_start, 0)
            lax.fori_loop(1, 16, lc_start, 0)

        @pl.when(i > 0)
        def _():
            send_pair(i - 1)

        return carry

    lax.fori_loop(0, 4, third, 0)
    dsib_copy(me_q).wait_recv()
    low = pl.multiple_of(h * OWN, OWN)
    gq_ref[...] = dq[me_q, pl.ds(low, OWN), :] + sib[me_q]
    send_pair(3)

    lax.fori_loop(1, 8, lr_arrive, 0)
    lax.fori_loop(1, 16, lc_arrive, 0)
    halves = []
    for s in range(2):
        halves.append(functools.reduce(jnp.add, [loss_r[s * 4 + k] for k in range(4)]))
    both = halves[0] + halves[1]
    halves = []
    for s in range(2):
        terms = [loss_c[xx * 4 + s * 2 + hh] for xx in range(4) for hh in range(2)]
        halves.append(functools.reduce(jnp.add, terms))
    both = both + (halves[0] + halves[1])
    both = jnp.sum(jnp.sum(both, axis=0, keepdims=True), axis=1, keepdims=True)
    loss_ref[...] = jnp.broadcast_to(both / (2.0 * 16384), (8, 128))

    def take_q(j, carry):
        other = (me_q + j) % NQ
        ref = inq.at[other]
        remote(ref, ref, gq_send.at[other], gq_recv.at[other], chip_peer(other)).wait_recv()
        gq_ref[...] += inq[other].astype(F32)
        return carry

    lax.fori_loop(1, NQ, take_q, 0)
    gq_ref[...] = 0.5 * (gq_ref[...] - 2.0 * p_ref[...].astype(F32))

    gp_ref[...] = dp[me_p % 2]

    def take_p(j, carry):
        other = (me_p + j) % NP
        ref = inp.at[other]
        remote(ref, ref, gp_send.at[other], gp_recv.at[other], col_peer(other)).wait_recv()
        gp_ref[...] += inp[other].astype(F32)
        return carry

    lax.fori_loop(1, NP, take_p, 0)
    gp_ref[...] = 0.5 * (gp_ref[...] - 2.0 * q_ref[...].astype(F32))

    for copy in q_sends + p_sends + q_fwd + p_fwd + sib_copies:
        copy.wait_send()

    def left_row(j, carry):
        to = (me_row + j) % 16
        tab_copy(me_row, to).wait_send()
        here = rstat.at[me_row]
        remote(here, here, rs_send.at[to], rs_recv.at[me_row], row_peer(to)).wait_send()
        here = loss_c.at[me_row]
        remote(here, here, lc_send.at[to], lc_recv.at[me_row], row_peer(to)).wait_send()
        return carry

    def left_col(j, carry):
        to = (me_p + j) % 8
        here = cstat.at[me_p]
        remote(here, here, cs_send.at[to], cs_recv.at[me_p], col_peer(to)).wait_send()
        here = loss_r.at[me_p]
        remote(here, here, lr_send.at[to], lr_recv.at[me_p], col_peer(to)).wait_send()
        gp_copy(to).wait_send()
        gq_copy((me_q + j) % 8).wait_send()
        return carry

    def left_sib(q, carry):
        dsib_copy(q).wait_send()
        return carry

    lax.fori_loop(1, 16, left_row, 0)
    lax.fori_loop(1, 8, left_col, 0)
    lax.fori_loop(0, 8, left_sib, 0)


def per_device(queries, passages, hard_ids, list_lengths):
    listed = hard_ids.shape[1]
    live = jnp.arange(listed, dtype=jnp.int32)[:, None] < list_lengths[None, :]
    ids = hard_ids.T
    owner, column = ids // OWN, ids % OWN
    core, zz = (owner // 16) % 2, (owner // 32 + 3) % 4
    xx, yy = (owner // 4) % 4, owner % 4
    dest = xx * 32 + (zz // 2) * 16 + core * 8 + (zz % 2) * 4 + yy
    dest = jnp.where(live, dest, -1)
    code = (column + 1).astype(F32)

    vm = pl.BlockSpec(memory_space=pltpu.VMEM)
    dma = pltpu.SemaphoreType.DMA
    loss, grad_queries, grad_passages = pl.pallas_call(
        kernel,
        out_shape=(
            jax.ShapeDtypeStruct((8, 128), F32),
            jax.ShapeDtypeStruct((OWN, D), F32),
            jax.ShapeDtypeStruct((OWN, D), F32),
        ),
        in_specs=[vm] * 4,
        out_specs=(vm, vm, vm),
        scratch_shapes=[
            pltpu.VMEM((NQ, QB, D), BF),
            pltpu.VMEM((NP, OWN, D), BF),
            pltpu.VMEM((NQ, QB, COLS), F32),
            pltpu.VMEM((NQ, QB, COLS), BF),
            pltpu.VMEM((NQ, QB, COLS), BF),
            pltpu.VMEM((128, 256), F32),
            pltpu.VMEM((16, 8, 256), F32),
            pltpu.VMEM((8, COLS), F32),
            pltpu.VMEM((8, COLS), F32),
            pltpu.VMEM((QB, 128), F32),
            pltpu.VMEM((16, 24, QB), F32),
            pltpu.VMEM((8, 2, COLS), F32),
            pltpu.VMEM((NQ, QB, 128), F32),
            pltpu.VMEM((8, COLS), F32),
            pltpu.VMEM((8, 8, 128), F32),
            pltpu.VMEM((16, 8, 128), F32),
            pltpu.VMEM((NQ, QB, D), F32),
            pltpu.VMEM((NQ, OWN, D), F32),
            pltpu.VMEM((NQ, OWN, D), BF),
            pltpu.VMEM((NQ, OWN, D), BF),
            pltpu.VMEM((2, OWN, D), F32),
            pltpu.VMEM((NP, OWN, D), BF),
            pltpu.VMEM((NP, OWN, D), BF),
            dma((8,)),
            dma((8,)),
            dma((8,)),
            dma((8,)),
            dma((8,)),
            dma((8,)),
            dma((16,)),
            dma((16,)),
            dma((16,)),
            dma((16,)),
            dma((8,)),
            dma((8,)),
            dma((8,)),
            dma((8,)),
            dma((16,)),
            dma((16,)),
            dma((8,)),
            dma((8,)),
            dma((8,)),
            dma((8,)),
            dma((8,)),
            dma((8,)),
        ],
        compiler_params=pltpu.CompilerParams(
            collective_id=0, has_side_effects=True, vmem_limit_bytes=60 * 1024 * 1024
        ),
        name="infonce",
    )(queries.astype(BF), passages.astype(BF), dest, code)
    return loss[0, 0], grad_queries, grad_passages


def solution(mesh):
    placed = (P(("pb", "pa"), None), P(("pb", "pa"), None), P(("pb", "pa"), None), P(("pb", "pa")))
    return jax.shard_map(
        per_device,
        mesh=mesh,
        in_specs=placed,
        out_specs=(P(), P(("pb", "pa"), None), P(("pb", "pa"), None)),
        check_vma=False,
    )
```

time: 496 us -> 108 us (0.22)
  waiting for transfers between devices: 125 us -> 0 us
  local copies, waits for them, and re-layouts: 125 us -> 3.76 us
  Pallas kernels: 0 us -> 99 us
  blocking collectives: 66.9 us -> 0 us
  matrix products: 55.7 us -> 0 us
  other arithmetic: 57 us -> 3.85 us
  starting transfers between devices: 47.6 us -> 0 us
  between operations: 17.6 us -> 0.65 us
    all_to_all x7 -> x0, waiting for transfers between devices: 125 us -> none  [the longest x1 64.7 us: per_device(): lax.all_to_all(found_rows, PB_PA, split_axis=0, concat_axis=0, tiled=True)]
    pallas_call x0 -> x1, Pallas kernels: none -> 99 us  [per_device(): pl.pallas_call(kernel, out_shape=(jax.ShapeDtypeStruct((8, 128), F32), ja...]
    scatter x3 -> x0, local copies, waits for them, and re-layouts: 67.7 us -> none  [the longest x1 28.6 us: per_device(): slot_weight = jnp.zeros((devices * capacity,), jnp.bfloat16).at[slot_plac...]
    dot_general x13 -> x0, matrix products: 55.7 us -> none  [the longest x4 21 us: query_piece_work(): return jnp.dot(weights, passage_block, preferred_element_type=jnp.float32)]
    all_to_all x7 -> x0, starting transfers between devices: 47.5 us -> none  [the longest x3 15.4 us: sent_to_all(): lax.all_to_all(jnp.broadcast_to(value[None], (size, *value.shape)), axis,...]
    psum x4 -> x0, blocking collectives: 46.4 us -> none  [by_axis(): return functools.reduce(lax.psum, axes, value)]
    gather x2 -> x0, local copies, waits for them, and re-layouts: 45.3 us -> none  [the longest x1 23.3 us: per_device(): fetched.reshape(devices * capacity, feature_width)[slot_place]]
    scatter-add x1 -> x0, other arithmetic: 34.5 us -> none  [per_device(): hard_passage = jnp.zeros((row_count, feature_width), jnp.float32).at[aske...]
  transfers between devices with their start and end apart: 9 -> 0, of which waited for: 5 -> 0; matrix products, arithmetic and copies ran while one was open for 38% -> 0% of each run, Pallas kernels for 0% -> 0%
where the time goes in v1:
time: 108 us; the launch traced here: 107 us
  Pallas kernels  99 us (92%)
  other arithmetic  3.85 us (4%)
  local copies, waits for them, and re-layouts  3.76 us (3%)
    pallas_call x1, Pallas kernels, per_device(): pl.pallas_call(kernel, out_shape=(jax.ShapeDtypeStruct((8, 128), F32), ja...  99 us
    unnamed x6, local copies, waits for them, and re-layouts  2.57 us

profile of v1, /device:TPU:0, one launch (start us, length us, event | category | flops | bytes accessed | tf_op | source)
XLA Modules:
  0.0 107.2 jit_solution(16654952029145616310)
XLA Ops:
  0.6 0.0 copy-start
  0.6 1.5 %fusion.16 = (f32[32,128]{1,0:T(8,128)}, s32[32,128]{1,0:T(8,128)}) fusion(s32[128,32]{0,1:T(8,128)} %param.6, s32[128]{0:T(128)} %param.7), kind=kLoop, calls=%fused_computation.46 | loop fusion | flops 503808 | bytes 49664 | tf_op jit(solution)/shard_map/convert_element_type | solution.py:628
  2.1 1.7 %convert_element_type.9.q_ref = bf16[128,768]{1,0:T(8,128)(2,1)} convert(f32[128,768]{1,0:T(8,128)} %param.4) | non-fusion elementwise | flops 98304 | bytes 589824 | tf_op jit(solution)/shard_map/convert_element_type | solution.py:692
  3.8 0.0 copy-done
  3.8 0.7 convert_element_type.10.p_ref
  4.5 99.0 %infonce.1 = (f32[8,128]{1,0:T(8,128)}, f32[128,768]{1,0:T(8,128)}, f32[128,768]{1,0:T(8,128)}) custom-call(bf16[128,768]{1,0:T(8,128)(2,1)} %convert_element_type.9.q_ref, bf16[128,768]{1,0:T(8,128)(2,1)} %convert_element_type.10.p_ref, s32[32,128]{1,0:T(8,128)} %get-tuple-element.10.dest_ref, f32[32,128]{1,0:T(8,128)} %get-tuple-element.9.code_ref), custom_call_target="tpu_custom_call" | custom-call | tf_op jit(solution)/shard_map/infonce/pallas_call | solution.py:632
  103.5 1.2 %slice.3 = f32[1,1]{1,0:T(1,128)} slice(f32[8,128]{1,0:T(8,128)} %get-tuple-element.6), slice={[0:1], [0:1]} | slice | bytes 8 | tf_op jit(solution)/shard_map/slice | solution.py:693
  104.7 0.0 copy-start.1
  104.7 1.8 %copy.9 = f32[128,768]{1,0:T(8,128)} copy(f32[128,768]{1,0:T(8,128)} %get-tuple-element.15) | data formatting | bytes 786432
  106.5 0.0 copy-done.1
  106.5 0.7 copy.10
Async XLA Ops:
  0.6 3.2 %copy-start = (f32[128,768]{1,0:T(8,128)S(1)}, f32[128,768]{1,0:T(8,128)}, u32[]{:S(2)}) copy-start(f32[128,768]{1,0:T(8,128)} %param.5) | copy-start | bytes 1179652
  104.7 1.8 %copy-start.1 = (f32[128,768]{1,0:T(8,128)S(1)}, f32[128,768]{1,0:T(8,128)}, u32[]{:S(2)}) copy-start(f32[128,768]{1,0:T(8,128)} %get-tuple-element.16) | copy-start | bytes 1179652

commit v2 on v1

--- a/solution.py
+++ b/solution.py
@@ -17,7 +17,7 @@
 QB = 256
 COLS = 1024
 ROWS = 2048
-CH = 32
+CH = 64
 NEG = float("-inf")
 
 
@@ -38,13 +38,17 @@
 
 
 def kernel(
+    queries_ref,
+    passages_ref,
+    ids_ref,
+    lengths_ref,
+    loss_ref,
+    gq_ref,
+    gp_ref,
     q_ref,
     p_ref,
     dest_ref,
     code_ref,
-    loss_ref,
-    gq_ref,
-    gp_ref,
     qbuf,
     pbuf,
     sbuf,
@@ -53,8 +57,11 @@
     table,
     tabs,
     cmax,
+    cnext,
     csum,
-    stat,
+    rnext,
+    wide_ref,
+    rsum,
     rstat,
     cstat,
     lrow,
@@ -144,6 +151,19 @@
 
     lax.fori_loop(1, 16, greet_row, 0)
     lax.fori_loop(1, 8, greet_col, 0)
+
+    q_ref[...] = queries_ref[...].astype(BF)
+    p_ref[...] = passages_ref[...].astype(BF)
+    ids = ids_ref[...]
+    owner = ids // OWN
+    third_z = (owner // 32 + 3) % 4
+    dest = (owner // 4) % 4 * 32 + (third_z // 2) * 16 + (owner // 16) % 2 * 8
+    dest = dest + (third_z % 2) * 4 + owner % 4
+    place = lax.broadcasted_iota(jnp.int32, ids.shape, 0)
+    dest_ref[...] = jnp.where(place < lengths_ref[...], dest, -1)
+    code_ref[...] = (ids % OWN + 1).astype(F32)
+    qbuf[me_q, pl.ds(pl.multiple_of(h * OWN, OWN), OWN), :] = q_ref[...]
+    pbuf[me_p] = p_ref[...]
     pl.semaphore_wait(barrier, 22)
 
     def q_at(xx, zz, first=0, size=OWN):
@@ -237,8 +257,6 @@
 
     sib_copies = [to_sibling(k, q_ref if k == 0 else None) for k in range(8)]
     sib_copies[0].start()
-    qbuf[me_q, pl.ds(pl.multiple_of(h * OWN, OWN), OWN), :] = q_ref[...]
-    pbuf[me_p] = p_ref[...]
 
     sub = lax.broadcasted_iota(jnp.int32, (128, 128), 0)
     lane = lax.broadcasted_iota(jnp.int32, (128, 128), 1)
@@ -263,6 +281,25 @@
         return count + both[:, 128:]
 
     lax.fori_loop(0, 32, slot_step, jnp.zeros((128, 128), F32), unroll=2)
+
+    def tab_copy(idx, to):
+        q, hh = to // 2, to % 2
+        zz = (pair * 2 + q % 2 + 3) % 4
+        group = (q // 2) * 4 + (zz // 2) * 2 + hh
+        return remote(
+            table.at[pl.ds(pl.multiple_of(group * 8, 8), 8), :],
+            tabs.at[idx],
+            tab_send.at[to],
+            tab_recv.at[idx],
+            row_peer(to),
+        )
+
+    def tab_start(j, carry):
+        tab_copy(me_row, (me_row + j) % 16).start()
+        return carry
+
+    lax.fori_loop(1, 16, tab_start, 0)
+    tabs[me_row] = table[pl.ds(pl.multiple_of((x * 4 + half * 2 + h) * 8, 8), 8), :]
 
     for k in range(3):
         q_wait[k].wait_recv()
@@ -279,25 +316,6 @@
             p_fwd[3].start()
         sib_copies[k + 1].start()
 
-    def tab_copy(idx, to):
-        q, hh = to // 2, to % 2
-        zz = (pair * 2 + q % 2 + 3) % 4
-        group = (q // 2) * 4 + (zz // 2) * 2 + hh
-        return remote(
-            table.at[pl.ds(pl.multiple_of(group * 8, 8), 8), :],
-            tabs.at[idx],
-            tab_send.at[to],
-            tab_recv.at[idx],
-            row_peer(to),
-        )
-
-    def tab_start(j, carry):
-        tab_copy(me_row, (me_row + j) % 16).start()
-        return carry
-
-    lax.fori_loop(1, 16, tab_start, 0)
-    tabs[me_row] = table[pl.ds(pl.multiple_of((x * 4 + half * 2 + h) * 8, 8), 8), :]
-
     for k in (3, 4):
         q_wait[k].wait_recv()
         p_wait[k].wait_recv()
@@ -333,51 +351,76 @@
         from_sibling(k).wait_recv()
 
     cmax[...] = jnp.full(cmax.shape, NEG, F32)
+    cnext[...] = jnp.full(cnext.shape, NEG, F32)
     csum[...] = jnp.zeros_like(csum)
-    first_half = lax.broadcasted_iota(jnp.int32, (CH, 128), 1) < 64
+    rnext[...] = jnp.full(rnext.shape, NEG, F32)
+
+    def scores(q, c):
+        cols = pl.ds(pl.multiple_of(c * 256, 256), 256)
+        part = dot_nt(qbuf[q], pbuf[pl.ds(2 * c, 2)].reshape(256, D))
+        sbuf[q, :, cols] = part
+        cnext[:, cols] = jnp.maximum(cnext[:, cols], eighths(part).max(0))
+        rnext[...] = jnp.maximum(rnext[...], jnp.maximum(part[:, :128], part[:, 128:]))
+
+    def levels():
+        csum[...] = csum[...] * jnp.exp(cmax[...] - cnext[...])
+        cmax[...] = cnext[...]
+        top = jnp.max(rnext[...], axis=1, keepdims=True)
+        wide_ref[...] = jnp.broadcast_to(top, (QB, 128))
+        rnext[...] = jnp.full(rnext.shape, NEG, F32)
+
+    def sums(q, r):
+        rows = pl.ds(pl.multiple_of(r * CH, CH), CH)
+        wide = wide_ref[rows, :]
+        total = jnp.zeros((CH, 128), F32)
+        for g in range(8):
+            cols = slice(g * 128, (g + 1) * 128)
+            s = sbuf[q, rows, cols]
+            e = jnp.exp(s - wide)
+            total += e + e * mbuf[q, rows, cols].astype(F32)
+            csum[:, cols] += jnp.exp(eighths(s) - cmax[:, cols][None]).sum(0)
+        rsum[rows, :] = total
+
+    def row_level(q):
+        top = wide_ref[...].T[0:1, :]
+        total = jnp.sum(rsum[...].T, axis=0, keepdims=True)
+        rstat[me_row, pl.ds(q, 1), :] = top + jnp.log(total)
+
+    def first_scores(c, carry):
+        scores(0, c)
+        return carry
+
+    lax.fori_loop(0, 4, first_scores, 0)
 
     def sweep(q, carry):
-        for c in range(4):
-            cols = slice(c * 256, (c + 1) * 256)
-            part = dot_nt(qbuf[q], pbuf[2 * c : 2 * c + 2].reshape(256, D))
-            sbuf[q, :, cols] = part
-            old = cmax[:, cols]
-            new = jnp.maximum(old, eighths(part).max(0))
-            csum[:, cols] = csum[:, cols] * jnp.exp(old - new)
-            cmax[:, cols] = new
-
-        def chunk(r, inner):
-            rows = pl.ds(pl.multiple_of(r * CH, CH), CH)
-            top = sbuf[q, rows, 0:128]
-            for g in range(1, 8):
-                top = jnp.maximum(top, sbuf[q, rows, g * 128 : (g + 1) * 128])
-            top = jnp.max(top, axis=1, keepdims=True)
-            wide = jnp.broadcast_to(top, (CH, 128))
-            total = jnp.zeros((CH, 128), F32)
-            for g in range(8):
-                cols = slice(g * 128, (g + 1) * 128)
-                s = sbuf[q, rows, cols]
-                e = jnp.exp(s - wide)
-                total += e + e * mbuf[q, rows, cols].astype(F32)
-                csum[:, cols] += jnp.exp(eighths(s) - cmax[:, cols][None]).sum(0)
-            total = jnp.sum(total, axis=1, keepdims=True)
-            stat[rows, :] = jnp.where(first_half, wide, total)
+        levels()
+
+        def step(c, inner):
+            sums(q, c)
+            scores(q + 1, c)
             return inner
 
-        lax.fori_loop(0, QB // CH, chunk, 0)
-        turned = stat[...].T
-        rstat[me_row, pl.ds(q, 1), :] = turned[0:1, :]
-        rstat[me_row, pl.ds(8 + q, 1), :] = turned[64:65, :]
-        return carry
-
-    lax.fori_loop(0, NQ, sweep, 0)
+        lax.fori_loop(0, 4, step, 0)
+        row_level(q)
+        return carry
+
+    lax.fori_loop(0, NQ - 1, sweep, 0)
+    levels()
+
+    def last_sums(c, carry):
+        sums(NQ - 1, c)
+        return carry
+
+    lax.fori_loop(0, 4, last_sums, 0)
+    row_level(NQ - 1)
 
     top = jnp.max(cmax[...], axis=0, keepdims=True)
-    cstat[me_p, 0:1, :] = top
-    cstat[me_p, 1:2, :] = jnp.sum(csum[...] * jnp.exp(cmax[...] - top), axis=0, keepdims=True)
-    diag = eighths(q_ref[...].astype(F32) * p_ref[...].astype(F32)).sum(0)
-    diag = diag[:, :256] + diag[:, 256:512] + diag[:, 512:]
-    rstat[me_row, 16:24, :] = diag
+    total = jnp.sum(csum[...] * jnp.exp(cmax[...] - top), axis=0, keepdims=True)
+    cstat[me_p, 0:1, :] = top + jnp.log(total)
+    diag = q_ref[...].astype(F32) * p_ref[...].astype(F32)
+    diag = jnp.sum(diag, axis=0, keepdims=True)
+    cstat[me_p, 1:2, 0:D] = diag
+    cstat[me_p, 1:2, D:COLS] = jnp.zeros((1, COLS - D), F32)
 
     def all_row(buf, send, recv):
         def start(j, carry):
@@ -411,34 +454,31 @@
 
     rs_start, rs_arrive = all_row(rstat, rs_send, rs_recv)
     cs_start, cs_arrive = all_col(cstat, cs_send, cs_recv)
+    lax.fori_loop(1, 16, rs_start, 0)
     lax.fori_loop(1, 8, cs_start, 0)
-    lax.fori_loop(1, 16, rs_start, 0)
     lax.fori_loop(1, 8, cs_arrive, 0)
 
-    tops = [cstat[k, 0:1, :] for k in range(8)]
-    peak = functools.reduce(jnp.maximum, tops)
-    total = functools.reduce(
-        jnp.add, [cstat[k, 1:2, :] * jnp.exp(tops[k] - peak) for k in range(8)]
-    )
+    parts = [cstat[k, 0:1, :] for k in range(8)]
+    peak = functools.reduce(jnp.maximum, parts)
+    total = functools.reduce(jnp.add, [jnp.exp(part - peak) for part in parts])
     column_lse = peak + jnp.log(total)
     lcol[...] = jnp.broadcast_to(column_lse, (8, COLS))
+    diag = functools.reduce(jnp.add, [cstat[k, 1:2, :] for k in range(8)])
+    part = column_lse - 2.0 * diag
+    part = functools.reduce(jnp.add, [part[:, g * 128 : (g + 1) * 128] for g in range(8)])
+    loss_c[me_row] = jnp.where(sub[:8] == 0, jnp.broadcast_to(part, (8, 128)), 0.0)
 
     lax.fori_loop(1, 16, rs_arrive, 0)
-    peak = rstat[0, 0:8, :]
+    peak = rstat[0]
     for k in range(1, 16):
-        peak = jnp.maximum(peak, rstat[k, 0:8, :])
+        peak = jnp.maximum(peak, rstat[k])
     total = jnp.zeros((8, QB), F32)
-    diag = jnp.zeros((8, QB), F32)
     for k in range(16):
-        total += rstat[k, 8:16, :] * jnp.exp(rstat[k, 0:8, :] - peak)
-        diag += rstat[k, 16:24, :]
+        total += jnp.exp(rstat[k] - peak)
     row_lse = peak + jnp.log(total)
     for q in range(NQ):
         lrow[q] = jnp.broadcast_to(row_lse[q : q + 1, :], (128, QB)).T
-    part = row_lse - 2.0 * diag
-    loss_r[me_p] = part[:, :128] + part[:, 128:]
-    part = functools.reduce(jnp.add, [column_lse[:, g * 128 : (g + 1) * 128] for g in range(8)])
-    loss_c[me_row] = jnp.where(sub[:8] == 0, jnp.broadcast_to(part, (8, 128)), 0.0)
+    loss_r[me_p] = row_lse[:, :128] + row_lse[:, 128:]
 
     def to_own(q):
         low = pl.multiple_of(h * OWN, OWN)
@@ -458,8 +498,8 @@
         return (me_q + 1 + i) % NQ
 
     def weights(q):
-        def chunk(r, inner):
-            rows = pl.ds(pl.multiple_of(r * CH, CH), CH)
+        for r in range(QB // CH):
+            rows = slice(r * CH, (r + 1) * CH)
             level = lrow[q, rows, :]
             for g in range(8):
                 cols = slice(g * 128, (g + 1) * 128)
@@ -470,9 +510,6 @@
                 hard_weight = er.astype(BF).astype(F32)
                 count = mbuf[q, rows, cols].astype(F32)
                 wbuf[q, rows, cols] = (pair_weight + count * hard_weight).astype(BF)
-            return inner
-
-        lax.fori_loop(0, QB // CH, chunk, 0)
 
     def query_sum(q):
         everything = pbuf[...].reshape(COLS, D)
@@ -485,27 +522,34 @@
         low = pl.multiple_of(h * OWN, OWN)
         outq[q] = (dq[q, pl.ds(low, OWN), :] + sib[q]).astype(BF)
 
+    lr_start, lr_arrive = all_col(loss_r, lr_send, lr_recv)
+    lc_start, lc_arrive = all_row(loss_c, lc_send, lc_recv)
+    weights(turn_q(0))
+    lax.fori_loop(1, 8, lr_start, 0)
+    lax.fori_loop(1, 16, lc_start, 0)
+
     def second(i, carry):
-        q = turn_q(i)
-        weights(q)
-
-        @pl.when(i > 0)
-        def _():
-            dsib_copy(turn_q(i - 1)).start()
-
         @pl.when(i > 1)
         def _():
-            gq_copy(turn_q(i - 2)).start()
-
-        query_sum(q)
-
-        @pl.when(i > 0)
+            dsib_copy(turn_q(i - 2)).start()
+
+        @pl.when(i > 4)
         def _():
-            take_sibling(turn_q(i - 1))
-
-        return carry
-
-    lax.fori_loop(0, NQ, second, 0)
+            gq_copy(turn_q(i - 5)).start()
+
+        query_sum(turn_q(i - 1))
+        weights(turn_q(i))
+
+        @pl.when(i > 3)
+        def _():
+            take_sibling(turn_q(i - 4))
+
+        return carry
+
+    lax.fori_loop(1, NQ, second, 0)
+    query_sum(turn_q(NQ - 1))
+    dsib_copy(turn_q(NQ - 2)).start()
+    gq_copy(turn_q(NQ - 5)).start()
 
     def turn_p(i):
         return (me_p // 2 + 1 + i) % 4
@@ -517,9 +561,6 @@
             @pl.when(p != me_p)
             def _():
                 gp_copy(p).start()
-
-    lr_start, lr_arrive = all_col(loss_r, lr_send, lr_recv)
-    lc_start, lc_arrive = all_row(loss_c, lc_send, lc_recv)
 
     def third(i, carry):
         block = turn_p(i)
@@ -533,9 +574,14 @@
         @pl.when(i == 0)
         def _():
             dsib_copy(turn_q(NQ - 1)).start()
-            gq_copy(turn_q(NQ - 2)).start()
-            lax.fori_loop(1, 8, lr_start, 0)
-            lax.fori_loop(1, 16, lc_start, 0)
+
+        @pl.when(i < 3)
+        def _():
+            take_sibling(turn_q(NQ - 4 + i))
+
+        @pl.when((i > 0) & (i < 4))
+        def _():
+            gq_copy(turn_q(NQ - 5 + i)).start()
 
         @pl.when(i > 0)
         def _():
@@ -548,6 +594,28 @@
     low = pl.multiple_of(h * OWN, OWN)
     gq_ref[...] = dq[me_q, pl.ds(low, OWN), :] + sib[me_q]
     send_pair(3)
+
+    def take_q(j, carry):
+        other = (me_q + j) % NQ
+        ref = inq.at[other]
+        remote(ref, ref, gq_send.at[other], gq_recv.at[other], chip_peer(other)).wait_recv()
+        gq_ref[...] += inq[other].astype(F32)
+        return carry
+
+    lax.fori_loop(1, NQ, take_q, 0)
+    gq_ref[...] = 0.5 * (gq_ref[...] - 2.0 * p_ref[...].astype(F32))
+
+    gp_ref[...] = dp[me_p % 2]
+
+    def take_p(j, carry):
+        other = (me_p + j) % NP
+        ref = inp.at[other]
+        remote(ref, ref, gp_send.at[other], gp_recv.at[other], col_peer(other)).wait_recv()
+        gp_ref[...] += inp[other].astype(F32)
+        return carry
+
+    lax.fori_loop(1, NP, take_p, 0)
+    gp_ref[...] = 0.5 * (gp_ref[...] - 2.0 * q_ref[...].astype(F32))
 
     lax.fori_loop(1, 8, lr_arrive, 0)
     lax.fori_loop(1, 16, lc_arrive, 0)
@@ -563,28 +631,6 @@
     both = jnp.sum(jnp.sum(both, axis=0, keepdims=True), axis=1, keepdims=True)
     loss_ref[...] = jnp.broadcast_to(both / (2.0 * 16384), (8, 128))
 
-    def take_q(j, carry):
-        other = (me_q + j) % NQ
-        ref = inq.at[other]
-        remote(ref, ref, gq_send.at[other], gq_recv.at[other], chip_peer(other)).wait_recv()
-        gq_ref[...] += inq[other].astype(F32)
-        return carry
-
-    lax.fori_loop(1, NQ, take_q, 0)
-    gq_ref[...] = 0.5 * (gq_ref[...] - 2.0 * p_ref[...].astype(F32))
-
-    gp_ref[...] = dp[me_p % 2]
-
-    def take_p(j, carry):
-        other = (me_p + j) % NP
-        ref = inp.at[other]
-        remote(ref, ref, gp_send.at[other], gp_recv.at[other], col_peer(other)).wait_recv()
-        gp_ref[...] += inp[other].astype(F32)
-        return carry
-
-    lax.fori_loop(1, NP, take_p, 0)
-    gp_ref[...] = 0.5 * (gp_ref[...] - 2.0 * q_ref[...].astype(F32))
-
     for copy in q_sends + p_sends + q_fwd + p_fwd + sib_copies:
         copy.wait_send()
 
@@ -617,16 +663,6 @@
 
 
 def per_device(queries, passages, hard_ids, list_lengths):
-    listed = hard_ids.shape[1]
-    live = jnp.arange(listed, dtype=jnp.int32)[:, None] < list_lengths[None, :]
-    ids = hard_ids.T
-    owner, column = ids // OWN, ids % OWN
-    core, zz = (owner // 16) % 2, (owner // 32 + 3) % 4
-    xx, yy = (owner // 4) % 4, owner % 4
-    dest = xx * 32 + (zz // 2) * 16 + core * 8 + (zz % 2) * 4 + yy
-    dest = jnp.where(live, dest, -1)
-    code = (column + 1).astype(F32)
-
     vm = pl.BlockSpec(memory_space=pltpu.VMEM)
     dma = pltpu.SemaphoreType.DMA
     loss, grad_queries, grad_passages = pl.pallas_call(
@@ -639,6 +675,10 @@
         in_specs=[vm] * 4,
         out_specs=(vm, vm, vm),
         scratch_shapes=[
+            pltpu.VMEM((OWN, D), BF),
+            pltpu.VMEM((OWN, D), BF),
+            pltpu.VMEM((32, OWN), jnp.int32),
+            pltpu.VMEM((32, OWN), F32),
             pltpu.VMEM((NQ, QB, D), BF),
             pltpu.VMEM((NP, OWN, D), BF),
             pltpu.VMEM((NQ, QB, COLS), F32),
@@ -648,8 +688,11 @@
             pltpu.VMEM((16, 8, 256), F32),
             pltpu.VMEM((8, COLS), F32),
             pltpu.VMEM((8, COLS), F32),
+            pltpu.VMEM((8, COLS), F32),
             pltpu.VMEM((QB, 128), F32),
-            pltpu.VMEM((16, 24, QB), F32),
+            pltpu.VMEM((QB, 128), F32),
+            pltpu.VMEM((QB, 128), F32),
+            pltpu.VMEM((16, 8, QB), F32),
             pltpu.VMEM((8, 2, COLS), F32),
             pltpu.VMEM((NQ, QB, 128), F32),
             pltpu.VMEM((8, COLS), F32),
@@ -689,7 +732,7 @@
             collective_id=0, has_side_effects=True, vmem_limit_bytes=60 * 1024 * 1024
         ),
         name="infonce",
-    )(queries.astype(BF), passages.astype(BF), dest, code)
+    )(queries, passages, hard_ids.T, list_lengths.reshape(1, OWN))
     return loss[0, 0], grad_queries, grad_passages
 
 

time: 108 us -> 87.1 us (0.81)
  Pallas kernels: 99 us -> 82.2 us
  other arithmetic: 3.85 us -> 0 us
    pallas_call x1, Pallas kernels: 99 us -> 82.2 us  [per_device(): pl.pallas_call(kernel, out_shape=(jax.ShapeDtypeStruct((8, 128), F32), ja...]
    convert_element_type x3 -> x0, other arithmetic: 3.85 us -> none  [the longest x1 1.69 us: per_device(): queries.astype(BF)]
    unnamed x6 -> x4, local copies, waits for them, and re-layouts: 2.57 us -> 2.57 us
where the time goes in v2:
time: 87.1 us; the launch traced here: 86.6 us
  Pallas kernels  82.2 us (94%)
  local copies, waits for them, and re-layouts  3.75 us (4%)
    pallas_call x1, Pallas kernels, per_device(): pl.pallas_call(kernel, out_shape=(jax.ShapeDtypeStruct((8, 128), F32), ja...  82.2 us
    unnamed x4, local copies, waits for them, and re-layouts  2.57 us

profile of v2, /device:TPU:0, one launch (start us, length us, event | category | flops | bytes accessed | tf_op | source)
XLA Modules:
  0.0 86.6 jit_solution(9062399343040680245)
XLA Ops:
  0.6 82.2 %infonce.1 = (f32[8,128]{1,0:T(8,128)}, f32[128,768]{1,0:T(8,128)}, f32[128,768]{1,0:T(8,128)}) custom-call(f32[128,768]{1,0:T(8,128)} %queries_ref.1, f32[128,768]{1,0:T(8,128)} %passages_ref.1, s32[32,128]{1,0:T(8,128)} %bitcast.3, s32[1,128]{1,0:T(1,128)} %bitcast.4), custom_call_target="tpu_custom_call" | custom-call | tf_op jit(solution)/shard_map/infonce/pallas_call | solution.py:668
  82.8 1.2 %slice.3 = f32[1,1]{1,0:T(1,128)} slice(f32[8,128]{1,0:T(8,128)} %get-tuple-element.6), slice={[0:1], [0:1]} | slice | bytes 8 | tf_op jit(solution)/shard_map/slice | solution.py:736
  84.0 0.0 copy-start
  84.0 1.8 %copy.9 = f32[128,768]{1,0:T(8,128)} copy(f32[128,768]{1,0:T(8,128)} %get-tuple-element.13) | data formatting | bytes 786432
  85.8 0.0 copy-done
  85.8 0.7 copy.10
Async XLA Ops:
  84.0 1.8 %copy-start = (f32[128,768]{1,0:T(8,128)S(1)}, f32[128,768]{1,0:T(8,128)}, u32[]{:S(2)}) copy-start(f32[128,768]{1,0:T(8,128)} %get-tuple-element.14) | copy-start | bytes 1179652

commit v3 on v2

v3 whole, which is shorter than its diff:
```python
import functools

import jax
import jax.numpy as jnp
from jax import lax
from jax.experimental import pallas as pl
from jax.experimental.pallas import tpu as pltpu
from jax.sharding import PartitionSpec as P

BF = jnp.bfloat16
F32 = jnp.float32
MESH = pl.DeviceIdType.MESH
D = 768
OWN = 128
NQ = 8
NP = 8
QB = 256
COLS = 1024
ROWS = 2048
CH = 64
PO, PL, PR, FAR, PAIR, LEFT, RIGHT, ME = range(8)
RING = (2, 3, 1, 2, 0, 3, 1, 0)
FLIP = (1, 1, 1, 0, 1, 0, 0, 0)
NEG = float("-inf")


def dot_nt(a, b):
    return lax.dot_general(a, b, (((1,), (1,)), ((), ())), preferred_element_type=F32)


def dot_nn(a, b):
    return lax.dot_general(a, b, (((1,), (0,)), ((), ())), preferred_element_type=F32)


def dot_tn(a, b):
    return lax.dot_general(a, b, (((0,), (0,)), ((), ())), preferred_element_type=F32)


def eighths(value):
    return value.reshape(value.shape[0] // 8, 8, value.shape[1])


def kernel(
    queries_hbm,
    passages_hbm,
    ids_hbm,
    lengths_hbm,
    loss_ref,
    gq_ref,
    gp_ref,
    queries_ref,
    passages_ref,
    ids_ref,
    lengths_ref,
    q_ref,
    p_ref,
    dest_ref,
    code_ref,
    qbuf,
    pbuf,
    sbuf,
    mbuf,
    wbuf,
    table,
    tabs,
    codes,
    cmax,
    cnext,
    csum,
    rnext,
    wide_ref,
    rsum,
    rstat,
    cstat,
    rlse,
    clse,
    lrow,
    lcol,
    loss_r,
    loss_c,
    dq,
    sib,
    dp,
    most,
    outq,
    inq,
    outq_scale,
    inq_scale,
    outp,
    inp,
    outp_scale,
    inp_scale,
    in_sem,
    q_send,
    q_recv,
    p_send,
    p_recv,
    sib_send,
    sib_recv,
    tab_send,
    tab_recv,
    rs_send,
    rs_recv,
    cs_send,
    cs_recv,
    lr_send,
    lr_recv,
    lc_send,
    lc_recv,
    dsib_send,
    dsib_recv,
    gq_send,
    gq_recv,
    gq_scale_send,
    gq_scale_recv,
    gp_send,
    gp_recv,
    gp_scale_send,
    gp_scale_recv,
):
    pb = lax.axis_index("pb")
    pa = lax.axis_index("pa")
    z, h = pb // 2, pb % 2
    x, y = pa // 4, pa % 4
    pair = z // 2
    zs = z % 2
    zc = (z + 3) % 4
    half, sel = zc // 2, zc % 2
    me_q = x * 2 + zs
    me_p = sel * 4 + y
    me_row = me_q * 2 + h

    def device(xx, yy, zz, hh):
        return (zz * 2 + hh, xx * 4 + yy)

    def row_peer(idx):
        q, hh = idx // 2, idx % 2
        return device(q // 2, y, pair * 2 + q % 2, hh)

    def col_peer(p):
        return device(x, p % 4, (half * 2 + p // 4 + 1) % 4, h)

    def q_index(k):
        return (x + RING[k]) % 4 * 2 + (1 - zs if FLIP[k] else zs)

    def p_index(k):
        return (1 - sel if FLIP[k] else sel) * 4 + (y + RING[k]) % 4

    sibling = device(x, y, z, 1 - h)
    mine = pl.ds(pl.multiple_of(h * OWN, OWN), OWN)
    others = pl.ds(pl.multiple_of((1 - h) * OWN, OWN), OWN)
    loads = [
        pltpu.make_async_copy(src, dst, in_sem.at[k])
        for k, (src, dst) in enumerate(
            [
                (queries_hbm, queries_ref),
                (passages_hbm, passages_ref),
                (ids_hbm, ids_ref),
                (lengths_hbm, lengths_ref),
            ]
        )
    ]
    for load in loads:
        load.start()

    def remote(src, dst, send, recv, to):
        return pltpu.make_async_remote_copy(
            src_ref=src,
            dst_ref=dst,
            send_sem=send,
            recv_sem=recv,
            device_id=to,
            device_id_type=MESH,
        )

    barrier = pltpu.get_barrier_semaphore()

    def greet_row(j, carry):
        pl.semaphore_signal(
            barrier, inc=1, device_id=row_peer((me_row + j) % 16), device_id_type=MESH
        )
        return carry

    def greet_col(j, carry):
        pl.semaphore_signal(
            barrier, inc=1, device_id=col_peer((me_p + j) % 8), device_id_type=MESH
        )
        return carry

    lax.fori_loop(1, 16, greet_row, 0)
    lax.fori_loop(1, 8, greet_col, 0)

    for load in loads:
        load.wait()
    q_ref[...] = queries_ref[...].astype(BF)
    p_ref[...] = passages_ref[...].astype(BF)
    ids = ids_ref[...]
    owner = ids // OWN
    third_z = (owner // 32 + 3) % 4
    dest = (owner // 4) % 4 * 32 + (third_z // 2) * 16 + (owner // 16) % 2 * 8
    dest = dest + (third_z % 2) * 4 + owner % 4
    place = lax.broadcasted_iota(jnp.int32, ids.shape, 0)
    dest_ref[...] = jnp.where(place < lengths_ref[...], dest, -1)
    code_ref[...] = (ids % OWN + 1).astype(F32)
    qbuf[ME, mine, :] = q_ref[...]
    pbuf[ME] = p_ref[...]
    pl.semaphore_wait(barrier, 22)

    def q_at(k, first=0, size=OWN):
        return qbuf.at[k, pl.ds(pl.multiple_of(h * OWN + first, 64), size), :]

    def p_at(k, first=0, size=OWN):
        return pbuf.at[k, pl.ds(first, size), :]

    def ring(at, own, to_left, to_right, to_pair, send, recv):
        plan = [
            (own, at(LEFT), to_right),
            (own, at(RIGHT), to_left),
            (own, at(PAIR), to_pair),
            (at(LEFT, 0, 64), at(FAR, 0, 64), to_right),
            (at(RIGHT, 64, 64), at(FAR, 64, 64), to_left),
            (at(PAIR), at(PL), to_right),
            (at(PAIR), at(PR), to_left),
            (at(FAR), at(PO), to_pair),
        ]
        return [
            remote(src, dst, send.at[k], recv.at[k], to) for k, (src, dst, to) in enumerate(plan)
        ]

    q_to = (
        device((x + 3) % 4, y, z, h),
        device((x + 1) % 4, y, z, h),
        device(x, y, pair * 2 + 1 - zs, h),
    )
    p_to = (
        device(x, (y + 3) % 4, z, h),
        device(x, (y + 1) % 4, z, h),
        device(x, y, (half * 2 + (1 - sel) + 1) % 4, h),
    )
    q_copies = ring(q_at, q_ref, *q_to, q_send, q_recv)
    p_copies = ring(p_at, p_ref, *p_to, p_send, p_recv)
    for k in range(3):
        q_copies[k].start()
        p_copies[k].start()

    sib_copies = [
        remote(q_ref if k == ME else q_at(k), q_at(k), sib_send.at[k], sib_recv.at[k], sibling)
        for k in range(8)
    ]
    sib_copies[ME].start()

    sub = lax.broadcasted_iota(jnp.int32, (128, 128), 0)
    lane = lax.broadcasted_iota(jnp.int32, (128, 128), 1)
    earlier = jnp.where(sub < lane, 1.0, 0.0).astype(BF)
    prefix = jnp.concatenate([earlier, jnp.ones((128, 128), BF)], axis=1)
    row_code = (lane + 1 + 128 * h).astype(F32)
    second_core = h.astype(F32)
    slot_of = (sub % 64).astype(F32)
    rows_here = jnp.where(sub < 64, 1.0 - second_core, second_core)
    table[...] = jnp.zeros_like(table)

    def slot_step(k, count):
        dest = dest_ref[pl.ds(k, 1), :]
        code = code_ref[pl.ds(k, 1), :]
        live = jnp.where(sub == dest, 1.0, 0.0)
        both = dot_nn(live.astype(BF), prefix)
        rank = jnp.sum(live * (both[:, :128] + count), axis=0, keepdims=True)
        value = rows_here * row_code + (1.0 - rows_here) * code
        chosen = jnp.where(slot_of == rank, value, 0.0).astype(BF)
        table[...] += dot_nt(live.astype(BF), chosen)
        return count + both[:, 128:]

    lax.fori_loop(0, 32, slot_step, jnp.zeros((128, 128), F32), unroll=4)

    def tab_copy(idx, to):
        q, hh = to // 2, to % 2
        zz = (pair * 2 + q % 2 + 3) % 4
        group = (q // 2) * 4 + (zz // 2) * 2 + hh
        return remote(
            table.at[pl.ds(pl.multiple_of(group * 8, 8), 8), :],
            tabs.at[idx],
            tab_send.at[to],
            tab_recv.at[idx],
            row_peer(to),
        )

    def tab_start(j, carry):
        tab_copy(me_row, (me_row + j) % 16).start()
        return carry

    lax.fori_loop(1, 16, tab_start, 0)
    tabs[me_row] = table[pl.ds(pl.multiple_of((x * 4 + half * 2 + h) * 8, 8), 8), :]

    for k, slot in ((0, LEFT), (1, RIGHT)):
        q_copies[k].wait_recv()
        q_copies[k + 3].start()
        p_copies[k].wait_recv()
        p_copies[k + 3].start()
        sib_copies[slot].start()
    q_copies[2].wait_recv()
    q_copies[5].start()
    q_copies[6].start()
    p_copies[2].wait_recv()
    p_copies[5].start()
    p_copies[6].start()
    sib_copies[PAIR].start()

    cmax[...] = jnp.full(cmax.shape, NEG, F32)
    cnext[...] = jnp.full(cnext.shape, NEG, F32)
    csum[...] = jnp.zeros_like(csum)
    rnext[...] = jnp.full(rnext.shape, NEG, F32)

    def scores(k, c):
        cols = slice(c * 256, (c + 1) * 256)
        part = dot_nt(qbuf[k], pbuf[2 * c : 2 * c + 2].reshape(256, D))
        sbuf[k, :, cols] = part
        cnext[:, cols] = jnp.maximum(cnext[:, cols], eighths(part).max(0))
        rnext[k] = jnp.maximum(rnext[k], jnp.maximum(part[:, :128], part[:, 128:]))

    for k in (ME, RIGHT, LEFT, PAIR):
        sib_copies[k].wait_recv()
        scores(k, 3)
        scores(k, 2)

    for k in (3, 4):
        q_copies[k].wait_recv()
        p_copies[k].wait_recv()
    q_copies[7].start()
    p_copies[7].start()
    sib_copies[FAR].start()

    def tab_arrive(j, carry):
        other = (me_row + j) % 16
        ref = tabs.at[other]
        remote(ref, ref, tab_send.at[other], tab_recv.at[other], row_peer(other)).wait_recv()
        return carry

    lax.fori_loop(1, 16, tab_arrive, 0)

    tall = (lax.broadcasted_iota(jnp.int32, (QB, 128), 0) + 1).astype(F32)
    near = lane[:8] < 64
    for k in range(8):
        first, last = tabs[2 * q_index(k)], tabs[2 * q_index(k) + 1]
        codes[k, 0:8, :] = jnp.where(near, first, last)
        codes[k, 8:16, :] = pltpu.roll(jnp.where(near, last, first), 64, 1)

    def count_step(k, carry):
        for p in range(NP):
            rows = codes[k, pl.ds(p_index(p), 1), :]
            cols = codes[k, pl.ds(p_index(p) + 8, 1), :]
            rows = jnp.where(tall == rows, 1.0, 0.0).astype(BF)
            cols = jnp.where(tall[:128] == cols, 1.0, 0.0).astype(BF)
            mbuf[k, :, p * 128 : (p + 1) * 128] = dot_nt(rows, cols).astype(BF)
        return carry

    lax.fori_loop(0, NQ, count_step, 0)
    sib_copies[FAR].wait_recv()
    scores(FAR, 3)
    scores(FAR, 2)

    for k, slot in ((5, PL), (6, PR), (7, PO)):
        q_copies[k].wait_recv()
        sib_copies[slot].start()
        p_copies[k].wait_recv()

    def levels(k):
        csum[...] = csum[...] * jnp.exp(cmax[...] - cnext[...])
        cmax[...] = cnext[...]
        top = jnp.max(rnext[k], axis=1, keepdims=True)
        wide_ref[k] = jnp.broadcast_to(top, (QB, 128))

    def sums(k, r):
        rows = slice(r * CH, (r + 1) * CH)
        wide = wide_ref[k, rows, :]
        total = jnp.zeros((CH, 128), F32)
        for g in range(8):
            cols = slice(g * 128, (g + 1) * 128)
            s = sbuf[k, rows, cols]
            e = jnp.exp(s - wide)
            total += e + e * mbuf[k, rows, cols].astype(F32)
            csum[:, cols] += jnp.exp(eighths(s) - cmax[:, cols][None]).sum(0)
        rsum[k, rows, :] = total

    def row_level(k):
        top = wide_ref[k].T[0:1, :]
        total = jnp.sum(rsum[k].T, axis=0, keepdims=True)
        rstat[me_row, pl.ds(q_index(k), 1), :] = top + jnp.log(total)

    turn = (ME, RIGHT, LEFT, PAIR, FAR, PR, PL, PO)
    scores(ME, 1)
    scores(ME, 0)
    for i, k in enumerate(turn):
        later = turn[i + 1] if i < 7 else None
        if later in (PR, PL, PO):
            sib_copies[later].wait_recv()
        levels(k)
        for r in range(4):
            sums(k, r)
            if later in (PR, PL, PO):
                scores(later, r)
            elif later is not None and r < 2:
                scores(later, r)
        row_level(k)

    top = jnp.max(cmax[...], axis=0, keepdims=True)
    total = jnp.sum(csum[...] * jnp.exp(cmax[...] - top), axis=0, keepdims=True)
    total = top + jnp.log(total)
    for p in range(NP):
        cstat[me_p, pl.ds(p_index(p), 1), :] = total[:, p * 128 : (p + 1) * 128]
    diag = eighths(q_ref[...].astype(F32) * p_ref[...].astype(F32)).sum(0)
    diag = functools.reduce(jnp.add, [diag[:, g * 128 : (g + 1) * 128] for g in range(6)])
    cstat[me_p, 8:16, :] = diag

    def all_row(buf, send, recv):
        def start(j, carry):
            to = (me_row + j) % 16
            here = buf.at[me_row]
            remote(here, here, send.at[to], recv.at[me_row], row_peer(to)).start()
            return carry

        def arrive(j, carry):
            other = (me_row + j) % 16
            ref = buf.at[other]
            remote(ref, ref, send.at[other], recv.at[other], row_peer(other)).wait_recv()
            return carry

        return start, arrive

    def all_col(buf, send, recv):
        def start(j, carry):
            to = (me_p + j) % 8
            here = buf.at[me_p]
            remote(here, here, send.at[to], recv.at[me_p], col_peer(to)).start()
            return carry

        def arrive(j, carry):
            other = (me_p + j) % 8
            ref = buf.at[other]
            remote(ref, ref, send.at[other], recv.at[other], col_peer(other)).wait_recv()
            return carry

        return start, arrive

    rs_start, rs_arrive = all_row(rstat, rs_send, rs_recv)
    cs_start, cs_arrive = all_col(cstat, cs_send, cs_recv)
    lax.fori_loop(1, 16, rs_start, 0)
    lax.fori_loop(1, 8, cs_start, 0)
    lax.fori_loop(1, 8, cs_arrive, 0)

    peak = functools.reduce(jnp.maximum, [cstat[k, 0:8, :] for k in range(8)])
    total = functools.reduce(jnp.add, [jnp.exp(cstat[k, 0:8, :] - peak) for k in range(8)])
    column_lse = peak + jnp.log(total)
    clse[...] = column_lse
    for p in range(NP):
        level = clse[pl.ds(p_index(p), 1), :]
        lcol[:, p * 128 : (p + 1) * 128] = jnp.broadcast_to(level, (8, 128))
    diag = functools.reduce(jnp.add, [cstat[k, 8:16, :] for k in range(8)])
    loss_c[me_row] = column_lse - 2.0 * diag

    lax.fori_loop(1, 16, rs_arrive, 0)
    peak = rstat[0]
    for k in range(1, 16):
        peak = jnp.maximum(peak, rstat[k])
    total = jnp.zeros((8, QB), F32)
    for k in range(16):
        total += jnp.exp(rstat[k] - peak)
    row_lse = peak + jnp.log(total)
    rlse[...] = row_lse
    for k in range(NQ):
        level = rlse[pl.ds(q_index(k), 1), :]
        lrow[k] = jnp.broadcast_to(level, (128, QB)).T
    loss_r[me_p] = row_lse[:, :128] + row_lse[:, 128:]

    def weights(k, c):
        for r in range(QB // CH):
            rows = slice(r * CH, (r + 1) * CH)
            level = lrow[k, rows, :]
            for g in (2 * c, 2 * c + 1):
                cols = slice(g * 128, (g + 1) * 128)
                s = sbuf[k, rows, cols]
                er = jnp.exp(s - level)
                ec = jnp.exp(eighths(s) - lcol[:, cols][None]).reshape(CH, 128)
                pair_weight = (er + ec).astype(BF).astype(F32)
                hard_weight = er.astype(BF).astype(F32)
                count = mbuf[k, rows, cols].astype(F32)
                wbuf[k, rows, cols] = (pair_weight + count * hard_weight).astype(BF)

    def query_sum(k, n):
        cols = slice(n * 256, (n + 1) * 256)
        dq[k, :, cols] = dot_nn(wbuf[k], pbuf[...].reshape(COLS, D)[:, cols])

    def passage_sums(c):
        left = wbuf[:, :, c * 256 : (c + 1) * 256].reshape(ROWS, 256)
        part = dot_tn(left, qbuf[...].reshape(ROWS, D))
        dp[2 * c : 2 * c + 2] = part.reshape(2, OWN, D)

    def dsib_copy(k):
        return remote(
            dq.at[k, others, :], sib.at[k], dsib_send.at[k], dsib_recv.at[k], sibling
        )

    def query_part(k):
        def rows(first, size):
            start = pl.multiple_of(h * OWN + first, 32)
            return dq[k, pl.ds(start, size), :] + sib[k, first : first + size, :]

        return rows

    def passage_part(p):
        return lambda first, size: dp[p, first : first + size, :]

    class Sums:
        def __init__(self, part, to, bufs, sems):
            to_left, to_right, to_pair = to
            self.part = part
            self.out, self.inn, self.out_scale, self.in_scale = bufs
            self.sems = sems
            self.block = {0: PO, 1: PL, 2: PR, 3: FAR, 5: PAIR, 6: LEFT, 7: RIGHT}
            self.to = (
                to_pair,
                to_left,
                to_right,
                to_left,
                to_right,
                to_pair,
                to_left,
                to_right,
            )

        def copies(self, k):
            send, recv, scale_send, scale_recv = self.sems
            src, dst = self.out.at[k], self.inn.at[k]
            scale = self.out_scale.at[k]
            if k in (3, 4):
                rows = pl.ds((k - 3) * 64, 64)
                src, dst, scale = self.out.at[3, rows, :], dst.at[rows, :], self.out_scale.at[3]
            return [
                remote(src, dst, send.at[k], recv.at[k], self.to[k]),
                remote(scale, self.in_scale.at[k], scale_send.at[k], scale_recv.at[k], self.to[k]),
            ]

        def start(self, *slots):
            for k in slots:
                for copy in self.copies(k):
                    copy.start()

        def arrive(self, *slots):
            for k in slots:
                for copy in self.copies(k):
                    copy.wait_recv()

        def levels(self, k):
            return jnp.broadcast_to(self.in_scale[k], (OWN, OWN)).T

        def decoded(self, k, level, first, size):
            value = self.inn[k, first : first + size, :].astype(jnp.int32).astype(F32)
            return value * jnp.concatenate([level[first : first + size]] * (D // OWN), axis=1)

        def encode(self, k, added=()):
            part = self.part(self.block[k])
            levels = {a: self.levels(a) for a, _, _ in added}
            for first in range(0, OWN, 32):
                value = part(first, 32)
                for a, low, high in added:
                    if low <= first < high:
                        value = value + self.decoded(a, levels[a], first, 32)
                top = jnp.max(jnp.abs(value), axis=1, keepdims=True)
                top = jnp.maximum(top, 1e-30)
                whole = jnp.round(value * (32766.0 / top)).astype(jnp.int32)
                self.out[k, first : first + 32, :] = whole.astype(jnp.int16)
                most[first : first + 32, :] = jnp.broadcast_to(top, (32, OWN))
            self.out_scale[k] = most[...].T[0:1, :] * (1.0 / 32766.0)

        def finish(self, grad, positive):
            part = self.part(ME)
            levels = {a: self.levels(a) for a in (5, 6, 7)}
            for first in range(0, OWN, 32):
                value = part(first, 32)
                for a in (5, 6, 7):
                    value = value + self.decoded(a, levels[a], first, 32)
                rows = slice(first, first + 32)
                grad[rows, :] = 0.5 * (value - 2.0 * positive[rows, :].astype(F32))

    qs = Sums(
        query_part,
        q_to,
        (outq, inq, outq_scale, inq_scale),
        (gq_send, gq_recv, gq_scale_send, gq_scale_recv),
    )
    ps = Sums(
        passage_part,
        p_to,
        (outp, inp, outp_scale, inp_scale),
        (gp_send, gp_recv, gp_scale_send, gp_scale_recv),
    )
    lr_start, lr_arrive = all_col(loss_r, lr_send, lr_recv)
    lc_start, lc_arrive = all_row(loss_c, lc_send, lc_recv)

    def both(k, *todo):
        for n in range(3):
            query_sum(k, n)
            for work in todo[n::3]:
                weights(*work)

    for c in range(4):
        weights(PO, c)
    both(PO, *[(PL, c) for c in range(4)])
    lax.fori_loop(1, 8, lr_start, 0)
    lax.fori_loop(1, 16, lc_start, 0)
    dsib_copy(PO).start()
    both(PL, *[(PR, c) for c in range(4)])
    dsib_copy(PL).start()
    rest = (FAR, PAIR, LEFT, RIGHT, ME)
    both(PR, *[(k, 0) for k in rest])
    dsib_copy(PO).wait_recv()
    qs.encode(0)
    dsib_copy(PR).start()
    passage_sums(0)
    for k in rest:
        weights(k, 1)
    qs.start(0)
    dsib_copy(PL).wait_recv()
    qs.encode(1)
    ps.encode(0)
    ps.encode(1)
    passage_sums(1)
    for k in rest:
        weights(k, 2)
    qs.start(1)
    ps.start(0, 1)
    dsib_copy(PR).wait_recv()
    qs.encode(2)
    ps.encode(2)
    for k in rest[:1]:
        weights(k, 3)
    both(FAR, *[(k, 3) for k in rest[1:]])
    qs.start(2)
    ps.start(2)
    query_sum(PAIR, 0)
    dsib_copy(FAR).start()
    query_sum(PAIR, 1)
    query_sum(PAIR, 2)
    passage_sums(2)
    dsib_copy(PAIR).start()
    both(LEFT)
    dsib_copy(FAR).wait_recv()
    qs.arrive(0)
    qs.encode(3, [(0, 0, OWN)])
    both(RIGHT)
    qs.start(3, 4)
    dsib_copy(LEFT).start()
    dsib_copy(PAIR).wait_recv()
    qs.arrive(1, 2)
    qs.encode(5, [(1, 0, OWN), (2, 0, OWN)])
    ps.arrive(0)
    ps.encode(3, [(0, 0, OWN)])
    both(ME)
    qs.start(5)
    ps.start(3, 4)
    dsib_copy(RIGHT).start()
    ps.arrive(1, 2)
    ps.encode(5, [(1, 0, OWN), (2, 0, OWN)])
    passage_sums(3)
    ps.start(5)
    dsib_copy(ME).start()
    dsib_copy(LEFT).wait_recv()
    qs.arrive(3)
    qs.encode(6, [(3, 0, 64)])
    dsib_copy(RIGHT).wait_recv()
    qs.arrive(4)
    qs.encode(7, [(4, 64, OWN)])
    qs.start(6, 7)
    ps.arrive(3)
    ps.encode(6, [(3, 0, 64)])
    ps.arrive(4)
    ps.encode(7, [(4, 64, OWN)])
    ps.start(6, 7)
    dsib_copy(ME).wait_recv()
    qs.arrive(5, 6, 7)
    qs.finish(gq_ref, p_ref)
    ps.arrive(5, 6, 7)
    ps.finish(gp_ref, q_ref)

    lax.fori_loop(1, 8, lr_arrive, 0)
    lax.fori_loop(1, 16, lc_arrive, 0)
    halves = []
    for s in range(2):
        halves.append(functools.reduce(jnp.add, [loss_r[s * 4 + k] for k in range(4)]))
    both = halves[0] + halves[1]
    halves = []
    for s in range(2):
        terms = [loss_c[xx * 4 + s * 2 + hh] for xx in range(4) for hh in range(2)]
        halves.append(functools.reduce(jnp.add, terms))
    both = both + (halves[0] + halves[1])
    both = jnp.sum(jnp.sum(both, axis=0, keepdims=True), axis=1, keepdims=True)
    loss_ref[...] = both / (2.0 * 16384)

    for side in (qs, ps):
        for k in range(8):
            for copy in side.copies(k):
                copy.wait_send()
    for copy in q_copies + p_copies + sib_copies:
        copy.wait_send()

    def left_row(j, carry):
        to = (me_row + j) % 16
        tab_copy(me_row, to).wait_send()
        here = rstat.at[me_row]
        remote(here, here, rs_send.at[to], rs_recv.at[me_row], row_peer(to)).wait_send()
        here = loss_c.at[me_row]
        remote(here, here, lc_send.at[to], lc_recv.at[me_row], row_peer(to)).wait_send()
        return carry

    def left_col(j, carry):
        to = (me_p + j) % 8
        here = cstat.at[me_p]
        remote(here, here, cs_send.at[to], cs_recv.at[me_p], col_peer(to)).wait_send()
        here = loss_r.at[me_p]
        remote(here, here, lr_send.at[to], lr_recv.at[me_p], col_peer(to)).wait_send()
        return carry

    def left_sib(q, carry):
        dsib_copy(q).wait_send()
        return carry

    lax.fori_loop(1, 16, left_row, 0)
    lax.fori_loop(1, 8, left_col, 0)
    lax.fori_loop(0, 8, left_sib, 0)


def per_device(queries, passages, hard_ids, list_lengths):
    vm = pl.BlockSpec(memory_space=pltpu.VMEM)
    dma = pltpu.SemaphoreType.DMA
    loss, grad_queries, grad_passages = pl.pallas_call(
        kernel,
        out_shape=(
            jax.ShapeDtypeStruct((1, 1), F32),
            jax.ShapeDtypeStruct((OWN, D), F32),
            jax.ShapeDtypeStruct((OWN, D), F32),
        ),
        in_specs=[pl.BlockSpec(memory_space=pltpu.HBM)] * 4,
        out_specs=(vm, vm, vm),
        scratch_shapes=[
            pltpu.VMEM((OWN, D), F32),
            pltpu.VMEM((OWN, D), F32),
            pltpu.VMEM((32, OWN), jnp.int32),
            pltpu.VMEM((1, OWN), jnp.int32),
            pltpu.VMEM((OWN, D), BF),
            pltpu.VMEM((OWN, D), BF),
            pltpu.VMEM((32, OWN), jnp.int32),
            pltpu.VMEM((32, OWN), F32),
            pltpu.VMEM((NQ, QB, D), BF),
            pltpu.VMEM((NP, OWN, D), BF),
            pltpu.VMEM((NQ, QB, COLS), F32),
            pltpu.VMEM((NQ, QB, COLS), BF),
            pltpu.VMEM((NQ, QB, COLS), BF),
            pltpu.VMEM((128, 128), F32),
            pltpu.VMEM((16, 8, 128), F32),
            pltpu.VMEM((NQ, 16, 128), F32),
            pltpu.VMEM((8, COLS), F32),
            pltpu.VMEM((8, COLS), F32),
            pltpu.VMEM((8, COLS), F32),
            pltpu.VMEM((NQ, QB, 128), F32),
            pltpu.VMEM((NQ, QB, 128), F32),
            pltpu.VMEM((NQ, QB, 128), F32),
            pltpu.VMEM((16, 8, QB), F32),
            pltpu.VMEM((8, 16, 128), F32),
            pltpu.VMEM((8, QB), F32),
            pltpu.VMEM((8, 128), F32),
            pltpu.VMEM((NQ, QB, 128), F32),
            pltpu.VMEM((8, COLS), F32),
            pltpu.VMEM((8, 8, 128), F32),
            pltpu.VMEM((16, 8, 128), F32),
            pltpu.VMEM((NQ, QB, D), F32),
            pltpu.VMEM((NQ, OWN, D), F32),
            pltpu.VMEM((NP, OWN, D), F32),
            pltpu.VMEM((OWN, OWN), F32),
            pltpu.VMEM((8, OWN, D), jnp.int16),
            pltpu.VMEM((8, OWN, D), jnp.int16),
            pltpu.VMEM((8, 1, OWN), F32),
            pltpu.VMEM((8, 1, OWN), F32),
            pltpu.VMEM((8, OWN, D), jnp.int16),
            pltpu.VMEM((8, OWN, D), jnp.int16),
            pltpu.VMEM((8, 1, OWN), F32),
            pltpu.VMEM((8, 1, OWN), F32),
            dma((4,)),
            dma((8,)),
            dma((8,)),
            dma((8,)),
            dma((8,)),
            dma((8,)),
            dma((8,)),
            dma((16,)),
            dma((16,)),
            dma((16,)),
            dma((16,)),
            dma((8,)),
            dma((8,)),
            dma((8,)),
            dma((8,)),
            dma((16,)),
            dma((16,)),
            dma((8,)),
            dma((8,)),
            dma((8,)),
            dma((8,)),
            dma((8,)),
            dma((8,)),
            dma((8,)),
            dma((8,)),
            dma((8,)),
            dma((8,)),
        ],
        compiler_params=pltpu.CompilerParams(
            collective_id=0, has_side_effects=True, vmem_limit_bytes=50 * 1024 * 1024
        ),
        name="infonce",
    )(queries, passages, hard_ids.T, list_lengths.reshape(1, OWN))
    return loss[0, 0], grad_queries, grad_passages


def solution(mesh):
    placed = (P(("pb", "pa"), None), P(("pb", "pa"), None), P(("pb", "pa"), None), P(("pb", "pa")))
    return jax.shard_map(
        per_device,
        mesh=mesh,
        in_specs=placed,
        out_specs=(P(), P(("pb", "pa"), None), P(("pb", "pa"), None)),
        check_vma=False,
    )
```

time: 87.1 us -> 75 us (0.86)
  Pallas kernels: 82.2 us -> 67.5 us
  between operations: 0.64 us -> 2.4 us
  local copies, waits for them, and re-layouts: 3.75 us -> 4.85 us
    pallas_call x1, Pallas kernels: 82.2 us -> 67.5 us  [per_device(): pl.pallas_call(kernel, out_shape=(jax.ShapeDtypeStruct((1, 1), F32), jax....]
    unnamed x4 -> x10, local copies, waits for them, and re-layouts: 2.57 us -> 4.85 us
    slice x1 -> x0, local copies, waits for them, and re-layouts: 1.18 us -> none  [per_device(): return (loss[0, 0], grad_queries, grad_passages)]
where the time goes in v3:
time: 75 us; the launch traced here: 74.7 us
  Pallas kernels  67.5 us (90%)
  local copies, waits for them, and re-layouts  4.85 us (6%)
  between operations  2.4 us (3%)
    pallas_call x1, Pallas kernels, per_device(): pl.pallas_call(kernel, out_shape=(jax.ShapeDtypeStruct((1, 1), F32), jax....  67.5 us
    unnamed x10, local copies, waits for them, and re-layouts  4.85 us

profile of v3, /device:TPU:0, one launch (start us, length us, event | category | flops | bytes accessed | tf_op | source)
XLA Modules:
  0.0 74.7 jit_solution(6054980759780024693)
XLA Ops:
  0.6 0.0 copy-start.3
  0.6 0.6 copy-done.3
  1.3 0.0 copy-start
  1.3 1.0 %copy-done = f32[128,768]{1,0:T(8,128)S(1)} copy-done((f32[128,768]{1,0:T(8,128)S(1)}, f32[128,768]{1,0:T(8,128)}, u32[]{:S(2)}) %copy-start) | copy-done | bytes 393240
  2.3 0.0 copy-start.1
  2.3 1.0 %copy-done.1 = f32[128,768]{1,0:T(8,128)S(1)} copy-done((f32[128,768]{1,0:T(8,128)S(1)}, f32[128,768]{1,0:T(8,128)}, u32[]{:S(2)}) %copy-start.1) | copy-done | bytes 393240
  3.3 0.0 copy-start.2
  3.3 0.7 copy-done.2
  4.0 67.5 %infonce.1 = (f32[1,1]{1,0:T(1,128)}, f32[128,768]{1,0:T(8,128)S(1)}, f32[128,768]{1,0:T(8,128)S(1)}) custom-call(f32[128,768]{1,0:T(8,128)S(1)} %copy-done, f32[128,768]{1,0:T(8,128)S(1)} %copy-done.1, s32[32,128]{1,0:T(8,128)S(1)} %bitcast.3, s32[1,128]{1,0:T(1,128)S(1)} %bitcast.4), custom_call_target="tpu_custom_call" | custom-call | tf_op jit(solution)/shard_map/infonce/pallas_call | solution.py:734
  72.1 0.7 %copy.11 = f32[128,768]{1,0:T(8,128)} copy(f32[128,768]{1,0:T(8,128)S(1)} %get-tuple-element.13) | data formatting | bytes 786432
  72.9 0.7 copy.12
Async XLA Ops:
  0.6 0.7 copy-start.3
  1.3 1.0 %copy-start = (f32[128,768]{1,0:T(8,128)S(1)}, f32[128,768]{1,0:T(8,128)}, u32[]{:S(2)}) copy-start(f32[128,768]{1,0:T(8,128)} %queries_hbm.1) | copy-start | bytes 1179652
  2.3 1.0 %copy-start.1 = (f32[128,768]{1,0:T(8,128)S(1)}, f32[128,768]{1,0:T(8,128)}, u32[]{:S(2)}) copy-start(f32[128,768]{1,0:T(8,128)} %passages_hbm.1) | copy-start | bytes 1179652
  3.3 0.7 copy-start.2

commit v4 on v3

--- a/solution.py
+++ b/solution.py
@@ -22,6 +22,8 @@
 RING = (2, 3, 1, 2, 0, 3, 1, 0)
 FLIP = (1, 1, 1, 0, 1, 0, 0, 0)
 NEG = float("-inf")
+LOG2E = 1.4426950408889634
+LN2 = 0.6931471805599453
 
 
 def dot_nt(a, b):
@@ -224,7 +226,7 @@
             (at(FAR), at(PO), to_pair),
         ]
         return [
-            remote(src, dst, send.at[k], recv.at[k], to) for k, (src, dst, to) in enumerate(plan)
+            remote(src, dst, send, recv.at[k], to) for k, (src, dst, to) in enumerate(plan)
         ]
 
     q_to = (
@@ -244,7 +246,7 @@
         p_copies[k].start()
 
     sib_copies = [
-        remote(q_ref if k == ME else q_at(k), q_at(k), sib_send.at[k], sib_recv.at[k], sibling)
+        remote(q_ref if k == ME else q_at(k), q_at(k), sib_send, sib_recv.at[k], sibling)
         for k in range(8)
     ]
     sib_copies[ME].start()
@@ -279,8 +281,8 @@
         return remote(
             table.at[pl.ds(pl.multiple_of(group * 8, 8), 8), :],
             tabs.at[idx],
-            tab_send.at[to],
-            tab_recv.at[idx],
+            tab_send,
+            tab_recv,
             row_peer(to),
         )
 
@@ -310,17 +312,21 @@
     csum[...] = jnp.zeros_like(csum)
     rnext[...] = jnp.full(rnext.shape, NEG, F32)
 
-    def scores(k, c):
+    def scores(k, slots, c):
         cols = slice(c * 256, (c + 1) * 256)
-        part = dot_nt(qbuf[k], pbuf[2 * c : 2 * c + 2].reshape(256, D))
-        sbuf[k, :, cols] = part
+        left = qbuf[k : k + slots].reshape(slots * QB, D)
+        part = dot_nt(left, pbuf[2 * c : 2 * c + 2].reshape(256, D)) * LOG2E
         cnext[:, cols] = jnp.maximum(cnext[:, cols], eighths(part).max(0))
-        rnext[k] = jnp.maximum(rnext[k], jnp.maximum(part[:, :128], part[:, 128:]))
-
-    for k in (ME, RIGHT, LEFT, PAIR):
+        for n in range(slots):
+            own = part[n * QB : (n + 1) * QB]
+            sbuf[k + n, :, cols] = own
+            rnext[k + n] = jnp.maximum(rnext[k + n], jnp.maximum(own[:, :128], own[:, 128:]))
+
+    for k in (RIGHT, PAIR):
         sib_copies[k].wait_recv()
-        scores(k, 3)
-        scores(k, 2)
+        sib_copies[k + 1].wait_recv()
+        scores(k, 2, 3)
+        scores(k, 2, 2)
 
     for k in (3, 4):
         q_copies[k].wait_recv()
@@ -329,13 +335,10 @@
     p_copies[7].start()
     sib_copies[FAR].start()
 
-    def tab_arrive(j, carry):
-        other = (me_row + j) % 16
-        ref = tabs.at[other]
-        remote(ref, ref, tab_send.at[other], tab_recv.at[other], row_peer(other)).wait_recv()
-        return carry
-
-    lax.fori_loop(1, 16, tab_arrive, 0)
+    def group(ref, send, recv):
+        return remote(ref, ref, send, recv, sibling)
+
+    group(tabs.at[0:15], tab_send, tab_recv).wait_recv()
 
     tall = (lax.broadcasted_iota(jnp.int32, (QB, 128), 0) + 1).astype(F32)
     near = lane[:8] < 64
@@ -355,8 +358,8 @@
 
     lax.fori_loop(0, NQ, count_step, 0)
     sib_copies[FAR].wait_recv()
-    scores(FAR, 3)
-    scores(FAR, 2)
+    scores(FAR, 1, 3)
+    scores(FAR, 1, 2)
 
     for k, slot in ((5, PL), (6, PR), (7, PO)):
         q_copies[k].wait_recv()
@@ -364,7 +367,7 @@
         p_copies[k].wait_recv()
 
     def levels(k):
-        csum[...] = csum[...] * jnp.exp(cmax[...] - cnext[...])
+        csum[...] = csum[...] * jnp.exp2(cmax[...] - cnext[...])
         cmax[...] = cnext[...]
         top = jnp.max(rnext[k], axis=1, keepdims=True)
         wide_ref[k] = jnp.broadcast_to(top, (QB, 128))
@@ -376,35 +379,42 @@
         for g in range(8):
             cols = slice(g * 128, (g + 1) * 128)
             s = sbuf[k, rows, cols]
-            e = jnp.exp(s - wide)
+            e = jnp.exp2(s - wide)
             total += e + e * mbuf[k, rows, cols].astype(F32)
-            csum[:, cols] += jnp.exp(eighths(s) - cmax[:, cols][None]).sum(0)
+            csum[:, cols] += jnp.exp2(eighths(s) - cmax[:, cols][None]).sum(0)
         rsum[k, rows, :] = total
 
     def row_level(k):
         top = wide_ref[k].T[0:1, :]
         total = jnp.sum(rsum[k].T, axis=0, keepdims=True)
-        rstat[me_row, pl.ds(q_index(k), 1), :] = top + jnp.log(total)
+        rstat[me_row, pl.ds(q_index(k), 1), :] = top + jnp.log2(total)
 
     turn = (ME, RIGHT, LEFT, PAIR, FAR, PR, PL, PO)
-    scores(ME, 1)
-    scores(ME, 0)
-    for i, k in enumerate(turn):
-        later = turn[i + 1] if i < 7 else None
-        if later in (PR, PL, PO):
-            sib_copies[later].wait_recv()
+    plan = {
+        ME: [(PAIR, 2, 1), (PAIR, 2, 0)],
+        LEFT: [(PR, 2, 1), (PR, 2, 0)],
+        FAR: [(PR, 1, 3), (PR, 1, 2)],
+        PAIR: [(PO, 2, 3), (PO, 2, 2)],
+        PR: [(PO, 2, 1), (PO, 2, 0)],
+    }
+    scores(RIGHT, 2, 1)
+    scores(RIGHT, 2, 0)
+    for k in turn:
+        if k == LEFT:
+            sib_copies[PR].wait_recv()
+        if k == PAIR:
+            sib_copies[PL].wait_recv()
+            sib_copies[PO].wait_recv()
         levels(k)
         for r in range(4):
             sums(k, r)
-            if later in (PR, PL, PO):
-                scores(later, r)
-            elif later is not None and r < 2:
-                scores(later, r)
+            if r % 2 and k in plan:
+                scores(*plan[k][r // 2])
         row_level(k)
 
     top = jnp.max(cmax[...], axis=0, keepdims=True)
-    total = jnp.sum(csum[...] * jnp.exp(cmax[...] - top), axis=0, keepdims=True)
-    total = top + jnp.log(total)
+    total = jnp.sum(csum[...] * jnp.exp2(cmax[...] - top), axis=0, keepdims=True)
+    total = top + jnp.log2(total)
     for p in range(NP):
         cstat[me_p, pl.ds(p_index(p), 1), :] = total[:, p * 128 : (p + 1) * 128]
     diag = eighths(q_ref[...].astype(F32) * p_ref[...].astype(F32)).sum(0)
@@ -413,63 +423,49 @@
 
     def all_row(buf, send, recv):
         def start(j, carry):
-            to = (me_row + j) % 16
             here = buf.at[me_row]
-            remote(here, here, send.at[to], recv.at[me_row], row_peer(to)).start()
+            remote(here, here, send, recv, row_peer((me_row + j) % 16)).start()
             return carry
 
-        def arrive(j, carry):
-            other = (me_row + j) % 16
-            ref = buf.at[other]
-            remote(ref, ref, send.at[other], recv.at[other], row_peer(other)).wait_recv()
-            return carry
-
-        return start, arrive
+        return start
 
     def all_col(buf, send, recv):
         def start(j, carry):
-            to = (me_p + j) % 8
             here = buf.at[me_p]
-            remote(here, here, send.at[to], recv.at[me_p], col_peer(to)).start()
+            remote(here, here, send, recv, col_peer((me_p + j) % 8)).start()
             return carry
 
-        def arrive(j, carry):
-            other = (me_p + j) % 8
-            ref = buf.at[other]
-            remote(ref, ref, send.at[other], recv.at[other], col_peer(other)).wait_recv()
-            return carry
-
-        return start, arrive
-
-    rs_start, rs_arrive = all_row(rstat, rs_send, rs_recv)
-    cs_start, cs_arrive = all_col(cstat, cs_send, cs_recv)
+        return start
+
+    rs_start = all_row(rstat, rs_send, rs_recv)
+    cs_start = all_col(cstat, cs_send, cs_recv)
     lax.fori_loop(1, 16, rs_start, 0)
     lax.fori_loop(1, 8, cs_start, 0)
-    lax.fori_loop(1, 8, cs_arrive, 0)
+    group(cstat.at[0:7], cs_send, cs_recv).wait_recv()
 
     peak = functools.reduce(jnp.maximum, [cstat[k, 0:8, :] for k in range(8)])
-    total = functools.reduce(jnp.add, [jnp.exp(cstat[k, 0:8, :] - peak) for k in range(8)])
-    column_lse = peak + jnp.log(total)
+    total = functools.reduce(jnp.add, [jnp.exp2(cstat[k, 0:8, :] - peak) for k in range(8)])
+    column_lse = peak + jnp.log2(total)
     clse[...] = column_lse
     for p in range(NP):
         level = clse[pl.ds(p_index(p), 1), :]
         lcol[:, p * 128 : (p + 1) * 128] = jnp.broadcast_to(level, (8, 128))
     diag = functools.reduce(jnp.add, [cstat[k, 8:16, :] for k in range(8)])
-    loss_c[me_row] = column_lse - 2.0 * diag
-
-    lax.fori_loop(1, 16, rs_arrive, 0)
+    loss_c[me_row] = LN2 * column_lse - 2.0 * diag
+
+    group(rstat.at[0:15], rs_send, rs_recv).wait_recv()
     peak = rstat[0]
     for k in range(1, 16):
         peak = jnp.maximum(peak, rstat[k])
     total = jnp.zeros((8, QB), F32)
     for k in range(16):
-        total += jnp.exp(rstat[k] - peak)
-    row_lse = peak + jnp.log(total)
+        total += jnp.exp2(rstat[k] - peak)
+    row_lse = peak + jnp.log2(total)
     rlse[...] = row_lse
     for k in range(NQ):
         level = rlse[pl.ds(q_index(k), 1), :]
         lrow[k] = jnp.broadcast_to(level, (128, QB)).T
-    loss_r[me_p] = row_lse[:, :128] + row_lse[:, 128:]
+    loss_r[me_p] = LN2 * (row_lse[:, :128] + row_lse[:, 128:])
 
     def weights(k, c):
         for r in range(QB // CH):
@@ -478,25 +474,33 @@
             for g in (2 * c, 2 * c + 1):
                 cols = slice(g * 128, (g + 1) * 128)
                 s = sbuf[k, rows, cols]
-                er = jnp.exp(s - level)
-                ec = jnp.exp(eighths(s) - lcol[:, cols][None]).reshape(CH, 128)
-                pair_weight = (er + ec).astype(BF).astype(F32)
-                hard_weight = er.astype(BF).astype(F32)
-                count = mbuf[k, rows, cols].astype(F32)
-                wbuf[k, rows, cols] = (pair_weight + count * hard_weight).astype(BF)
-
-    def query_sum(k, n):
-        cols = slice(n * 256, (n + 1) * 256)
-        dq[k, :, cols] = dot_nn(wbuf[k], pbuf[...].reshape(COLS, D)[:, cols])
+                er = jnp.exp2(s - level)
+                ec = jnp.exp2(eighths(s) - lcol[:, cols][None]).reshape(CH, 128)
+                pair_weight = (er + ec).astype(BF)
+                hard_weight = er.astype(BF)
+                wbuf[k, rows, cols] = pair_weight + mbuf[k, rows, cols] * hard_weight
+
+    def query_sums(k, slots):
+        def part(n):
+            cols = slice(n * 256, (n + 1) * 256)
+            left = wbuf[k : k + slots].reshape(slots * QB, COLS)
+            found = dot_nn(left, pbuf[...].reshape(COLS, D)[:, cols])
+            dq[k : k + slots, :, cols] = found.reshape(slots, QB, 256)
+
+        return part
 
     def passage_sums(c):
-        left = wbuf[:, :, c * 256 : (c + 1) * 256].reshape(ROWS, 256)
-        part = dot_tn(left, qbuf[...].reshape(ROWS, D))
-        dp[2 * c : 2 * c + 2] = part.reshape(2, OWN, D)
+        def part(n):
+            cols = slice(n * 256, (n + 1) * 256)
+            left = wbuf[:, :, c * 256 : (c + 1) * 256].reshape(ROWS, 256)
+            found = dot_tn(left, qbuf[...].reshape(ROWS, D)[:, cols])
+            dp[2 * c : 2 * c + 2, :, cols] = found.reshape(2, OWN, 256)
+
+        return part
 
     def dsib_copy(k):
         return remote(
-            dq.at[k, others, :], sib.at[k], dsib_send.at[k], dsib_recv.at[k], sibling
+            dq.at[k, others, :], sib.at[k], dsib_send, dsib_recv.at[k], sibling
         )
 
     def query_part(k):
@@ -515,28 +519,29 @@
             self.part = part
             self.out, self.inn, self.out_scale, self.in_scale = bufs
             self.sems = sems
-            self.block = {0: PO, 1: PL, 2: PR, 3: FAR, 5: PAIR, 6: LEFT, 7: RIGHT}
-            self.to = (
-                to_pair,
-                to_left,
-                to_right,
-                to_left,
-                to_right,
-                to_pair,
-                to_left,
-                to_right,
+            self.slots = (
+                (PO, 0, OWN, to_pair),
+                (PL, 0, OWN, to_left),
+                (PR, 0, OWN, to_right),
+                (FAR, 0, 64, to_left),
+                (FAR, 64, OWN, to_right),
+                (PAIR, 0, OWN, to_pair),
+                (LEFT, 64, OWN, to_left),
+                (RIGHT, 0, 64, to_right),
+                (LEFT, 0, 64, to_left),
+                (RIGHT, 64, OWN, to_right),
             )
 
         def copies(self, k):
             send, recv, scale_send, scale_recv = self.sems
+            _, low, high, to = self.slots[k]
             src, dst = self.out.at[k], self.inn.at[k]
-            scale = self.out_scale.at[k]
-            if k in (3, 4):
-                rows = pl.ds((k - 3) * 64, 64)
-                src, dst, scale = self.out.at[3, rows, :], dst.at[rows, :], self.out_scale.at[3]
+            if high - low < OWN:
+                src, dst = src.at[pl.ds(low, high - low), :], dst.at[pl.ds(low, high - low), :]
+            scale, scale_dst = self.out_scale.at[k], self.in_scale.at[k]
             return [
-                remote(src, dst, send.at[k], recv.at[k], self.to[k]),
-                remote(scale, self.in_scale.at[k], scale_send.at[k], scale_recv.at[k], self.to[k]),
+                remote(src, dst, send, recv.at[k], to),
+                remote(scale, scale_dst, scale_send, scale_recv.at[k], to),
             ]
 
         def start(self, *slots):
@@ -557,13 +562,13 @@
             return value * jnp.concatenate([level[first : first + size]] * (D // OWN), axis=1)
 
         def encode(self, k, added=()):
-            part = self.part(self.block[k])
-            levels = {a: self.levels(a) for a, _, _ in added}
-            for first in range(0, OWN, 32):
+            block, low, high, _ = self.slots[k]
+            part = self.part(block)
+            levels = {a: self.levels(a) for a in added}
+            for first in range(low, high, 32):
                 value = part(first, 32)
-                for a, low, high in added:
-                    if low <= first < high:
-                        value = value + self.decoded(a, levels[a], first, 32)
+                for a in added:
+                    value = value + self.decoded(a, levels[a], first, 32)
                 top = jnp.max(jnp.abs(value), axis=1, keepdims=True)
                 top = jnp.maximum(top, 1e-30)
                 whole = jnp.round(value * (32766.0 / top)).astype(jnp.int32)
@@ -573,11 +578,12 @@
 
         def finish(self, grad, positive):
             part = self.part(ME)
-            levels = {a: self.levels(a) for a in (5, 6, 7)}
+            levels = {a: self.levels(a) for a in range(5, 10)}
             for first in range(0, OWN, 32):
                 value = part(first, 32)
-                for a in (5, 6, 7):
-                    value = value + self.decoded(a, levels[a], first, 32)
+                for a in range(5, 10):
+                    if self.slots[a][1] <= first < self.slots[a][2]:
+                        value = value + self.decoded(a, levels[a], first, 32)
                 rows = slice(first, first + 32)
                 grad[rows, :] = 0.5 * (value - 2.0 * positive[rows, :].astype(F32))
 
@@ -593,96 +599,94 @@
         (outp, inp, outp_scale, inp_scale),
         (gp_send, gp_recv, gp_scale_send, gp_scale_recv),
     )
-    lr_start, lr_arrive = all_col(loss_r, lr_send, lr_recv)
-    lc_start, lc_arrive = all_row(loss_c, lc_send, lc_recv)
-
-    def both(k, *todo):
+    lr_start = all_col(loss_r, lr_send, lr_recv)
+    lc_start = all_row(loss_c, lc_send, lc_recv)
+
+    def beside(part, todo=()):
         for n in range(3):
-            query_sum(k, n)
+            part(n)
             for work in todo[n::3]:
                 weights(*work)
 
-    for c in range(4):
-        weights(PO, c)
-    both(PO, *[(PL, c) for c in range(4)])
-    lax.fori_loop(1, 8, lr_start, 0)
-    lax.fori_loop(1, 16, lc_start, 0)
+    def every(slots, columns):
+        return [(k, c) for k in slots for c in columns]
+
+    most[...] = jnp.ones_like(most)
+    rest = (FAR, PAIR, LEFT, RIGHT, ME)
+    for work in every((PO, PL, PR), range(4)):
+        weights(*work)
+    beside(query_sums(PO, 3), every(rest, (0, 1)))
     dsib_copy(PO).start()
-    both(PL, *[(PR, c) for c in range(4)])
     dsib_copy(PL).start()
-    rest = (FAR, PAIR, LEFT, RIGHT, ME)
-    both(PR, *[(k, 0) for k in rest])
+    dsib_copy(PR).start()
+    beside(passage_sums(0), every(rest, (2, 3)))
     dsib_copy(PO).wait_recv()
     qs.encode(0)
-    dsib_copy(PR).start()
-    passage_sums(0)
-    for k in rest:
-        weights(k, 1)
+    ps.encode(0)
+    ps.encode(1)
     qs.start(0)
+    ps.start(0, 1)
     dsib_copy(PL).wait_recv()
     qs.encode(1)
-    ps.encode(0)
-    ps.encode(1)
-    passage_sums(1)
-    for k in rest:
-        weights(k, 2)
+    beside(passage_sums(1))
     qs.start(1)
-    ps.start(0, 1)
     dsib_copy(PR).wait_recv()
     qs.encode(2)
     ps.encode(2)
-    for k in rest[:1]:
-        weights(k, 3)
-    both(FAR, *[(k, 3) for k in rest[1:]])
     qs.start(2)
     ps.start(2)
-    query_sum(PAIR, 0)
-    dsib_copy(FAR).start()
-    query_sum(PAIR, 1)
-    query_sum(PAIR, 2)
-    passage_sums(2)
-    dsib_copy(PAIR).start()
-    both(LEFT)
+    beside(query_sums(FAR, 2))
+    beside(query_sums(LEFT, 2))
+    for k in (FAR, PAIR, LEFT, RIGHT):
+        dsib_copy(k).start()
+    beside(passage_sums(2))
     dsib_copy(FAR).wait_recv()
     qs.arrive(0)
-    qs.encode(3, [(0, 0, OWN)])
-    both(RIGHT)
+    qs.encode(3, [0])
+    qs.encode(4, [0])
     qs.start(3, 4)
-    dsib_copy(LEFT).start()
+    ps.arrive(0)
+    ps.encode(3, [0])
+    ps.encode(4, [0])
+    ps.start(3, 4)
+    dsib_copy(LEFT).wait_recv()
+    qs.encode(6)
+    dsib_copy(RIGHT).wait_recv()
+    qs.encode(7)
+    beside(passage_sums(3))
+    qs.start(6, 7)
     dsib_copy(PAIR).wait_recv()
     qs.arrive(1, 2)
-    qs.encode(5, [(1, 0, OWN), (2, 0, OWN)])
-    ps.arrive(0)
-    ps.encode(3, [(0, 0, OWN)])
-    both(ME)
+    qs.encode(5, [1, 2])
+    ps.encode(6)
+    ps.encode(7)
     qs.start(5)
-    ps.start(3, 4)
-    dsib_copy(RIGHT).start()
     ps.arrive(1, 2)
-    ps.encode(5, [(1, 0, OWN), (2, 0, OWN)])
-    passage_sums(3)
+    ps.encode(5, [1, 2])
+    ps.start(6, 7)
+    beside(query_sums(ME, 1))
     ps.start(5)
     dsib_copy(ME).start()
-    dsib_copy(LEFT).wait_recv()
+    lax.fori_loop(1, 8, lr_start, 0)
+    lax.fori_loop(1, 16, lc_start, 0)
     qs.arrive(3)
-    qs.encode(6, [(3, 0, 64)])
-    dsib_copy(RIGHT).wait_recv()
+    qs.encode(8, [3])
     qs.arrive(4)
-    qs.encode(7, [(4, 64, OWN)])
-    qs.start(6, 7)
+    qs.encode(9, [4])
+    qs.start(8, 9)
     ps.arrive(3)
-    ps.encode(6, [(3, 0, 64)])
+    ps.encode(8, [3])
     ps.arrive(4)
-    ps.encode(7, [(4, 64, OWN)])
-    ps.start(6, 7)
+    ps.encode(9, [4])
+    ps.start(8, 9)
     dsib_copy(ME).wait_recv()
-    qs.arrive(5, 6, 7)
+    qs.arrive(5, 6, 7, 8, 9)
     qs.finish(gq_ref, p_ref)
-    ps.arrive(5, 6, 7)
+    ps.arrive(5, 6, 7, 8, 9)
     ps.finish(gp_ref, q_ref)
 
-    lax.fori_loop(1, 8, lr_arrive, 0)
-    lax.fori_loop(1, 16, lc_arrive, 0)
+    group(loss_r.at[0:7], lr_send, lr_recv).wait_recv()
+    group(loss_c.at[0:15], lc_send, lc_recv).wait_recv()
     halves = []
     for s in range(2):
         halves.append(functools.reduce(jnp.add, [loss_r[s * 4 + k] for k in range(4)]))
@@ -695,37 +699,19 @@
     both = jnp.sum(jnp.sum(both, axis=0, keepdims=True), axis=1, keepdims=True)
     loss_ref[...] = both / (2.0 * 16384)
 
-    for side in (qs, ps):
-        for k in range(8):
-            for copy in side.copies(k):
-                copy.wait_send()
-    for copy in q_copies + p_copies + sib_copies:
-        copy.wait_send()
-
-    def left_row(j, carry):
-        to = (me_row + j) % 16
-        tab_copy(me_row, to).wait_send()
-        here = rstat.at[me_row]
-        remote(here, here, rs_send.at[to], rs_recv.at[me_row], row_peer(to)).wait_send()
-        here = loss_c.at[me_row]
-        remote(here, here, lc_send.at[to], lc_recv.at[me_row], row_peer(to)).wait_send()
-        return carry
-
-    def left_col(j, carry):
-        to = (me_p + j) % 8
-        here = cstat.at[me_p]
-        remote(here, here, cs_send.at[to], cs_recv.at[me_p], col_peer(to)).wait_send()
-        here = loss_r.at[me_p]
-        remote(here, here, lr_send.at[to], lr_recv.at[me_p], col_peer(to)).wait_send()
-        return carry
-
-    def left_sib(q, carry):
-        dsib_copy(q).wait_send()
-        return carry
-
-    lax.fori_loop(1, 16, left_row, 0)
-    lax.fori_loop(1, 8, left_col, 0)
-    lax.fori_loop(0, 8, left_sib, 0)
+    group(pbuf.at[0:7], q_send, q_recv.at[0]).wait_send()
+    group(pbuf.at[0:7], p_send, p_recv.at[0]).wait_send()
+    group(pbuf, sib_send, sib_recv.at[0]).wait_send()
+    group(tabs.at[0:15], tab_send, tab_recv).wait_send()
+    group(rstat.at[0:15], rs_send, rs_recv).wait_send()
+    group(cstat.at[0:7], cs_send, cs_recv).wait_send()
+    group(loss_r.at[0:7], lr_send, lr_recv).wait_send()
+    group(loss_c.at[0:15], lc_send, lc_recv).wait_send()
+    group(sib, dsib_send, dsib_recv.at[0]).wait_send()
+    group(outq.at[0:7], gq_send, gq_recv.at[0]).wait_send()
+    group(outp.at[0:7], gp_send, gp_recv.at[0]).wait_send()
+    group(outq_scale, gq_scale_send, gq_scale_recv.at[0]).wait_send()
+    group(outp_scale, gp_scale_send, gp_scale_recv.at[0]).wait_send()
 
 
 def per_device(queries, passages, hard_ids, list_lengths):
@@ -775,41 +761,41 @@
             pltpu.VMEM((NQ, OWN, D), F32),
             pltpu.VMEM((NP, OWN, D), F32),
             pltpu.VMEM((OWN, OWN), F32),
-            pltpu.VMEM((8, OWN, D), jnp.int16),
-            pltpu.VMEM((8, OWN, D), jnp.int16),
-            pltpu.VMEM((8, 1, OWN), F32),
-            pltpu.VMEM((8, 1, OWN), F32),
-            pltpu.VMEM((8, OWN, D), jnp.int16),
-            pltpu.VMEM((8, OWN, D), jnp.int16),
-            pltpu.VMEM((8, 1, OWN), F32),
-            pltpu.VMEM((8, 1, OWN), F32),
+            pltpu.VMEM((10, OWN, D), jnp.int16),
+            pltpu.VMEM((10, OWN, D), jnp.int16),
+            pltpu.VMEM((10, 1, OWN), F32),
+            pltpu.VMEM((10, 1, OWN), F32),
+            pltpu.VMEM((10, OWN, D), jnp.int16),
+            pltpu.VMEM((10, OWN, D), jnp.int16),
+            pltpu.VMEM((10, 1, OWN), F32),
+            pltpu.VMEM((10, 1, OWN), F32),
             dma((4,)),
+            dma,
             dma((8,)),
+            dma,
             dma((8,)),
+            dma,
             dma((8,)),
+            dma,
+            dma,
+            dma,
+            dma,
+            dma,
+            dma,
+            dma,
+            dma,
+            dma,
+            dma,
+            dma,
             dma((8,)),
-            dma((8,)),
-            dma((8,)),
-            dma((16,)),
-            dma((16,)),
-            dma((16,)),
-            dma((16,)),
-            dma((8,)),
-            dma((8,)),
-            dma((8,)),
-            dma((8,)),
-            dma((16,)),
-            dma((16,)),
-            dma((8,)),
-            dma((8,)),
-            dma((8,)),
-            dma((8,)),
-            dma((8,)),
-            dma((8,)),
-            dma((8,)),
-            dma((8,)),
-            dma((8,)),
-            dma((8,)),
+            dma,
+            dma((10,)),
+            dma,
+            dma((10,)),
+            dma,
+            dma((10,)),
+            dma,
+            dma((10,)),
         ],
         compiler_params=pltpu.CompilerParams(
             collective_id=0, has_side_effects=True, vmem_limit_bytes=50 * 1024 * 1024

time: 75 us -> 66.4 us (0.89)
  Pallas kernels: 67.5 us -> 58.9 us
    pallas_call x1, Pallas kernels: 67.5 us -> 58.9 us  [per_device(): pl.pallas_call(kernel, out_shape=(jax.ShapeDtypeStruct((1, 1), F32), jax....]
where the time goes in v4:
time: 66.4 us; the launch traced here: 66.2 us
  Pallas kernels  58.9 us (89%)
  local copies, waits for them, and re-layouts  4.85 us (7%)
  between operations  2.4 us (4%)
    pallas_call x1, Pallas kernels, per_device(): pl.pallas_call(kernel, out_shape=(jax.ShapeDtypeStruct((1, 1), F32), jax....  58.9 us
    unnamed x10, local copies, waits for them, and re-layouts  4.85 us

profile of v4, /device:TPU:0, one launch (start us, length us, event | category | flops | bytes accessed | tf_op | source)
XLA Modules:
  0.0 66.2 jit_solution(9678861504021458180)
XLA Ops:
  0.6 0.0 copy-start.3
  0.6 0.6 copy-done.3
  1.3 0.0 copy-start
  1.3 1.0 %copy-done = f32[128,768]{1,0:T(8,128)S(1)} copy-done((f32[128,768]{1,0:T(8,128)S(1)}, f32[128,768]{1,0:T(8,128)}, u32[]{:S(2)}) %copy-start) | copy-done | bytes 393240
  2.3 0.0 copy-start.1
  2.3 1.0 %copy-done.1 = f32[128,768]{1,0:T(8,128)S(1)} copy-done((f32[128,768]{1,0:T(8,128)S(1)}, f32[128,768]{1,0:T(8,128)}, u32[]{:S(2)}) %copy-start.1) | copy-done | bytes 393240
  3.3 0.0 copy-start.2
  3.3 0.7 %copy-done.2 = s32[128,32]{0,1:T(8,128)S(1)} copy-done((s32[128,32]{0,1:T(8,128)S(1)}, s32[128,32]{0,1:T(8,128)}, u32[]{:S(2)}) %copy-start.2) | copy-done | bytes 16408
  4.0 58.9 %infonce.1 = (f32[1,1]{1,0:T(1,128)}, f32[128,768]{1,0:T(8,128)S(1)}, f32[128,768]{1,0:T(8,128)S(1)}) custom-call(f32[128,768]{1,0:T(8,128)S(1)} %copy-done, f32[128,768]{1,0:T(8,128)S(1)} %copy-done.1, s32[32,128]{1,0:T(8,128)S(1)} %bitcast.3, s32[1,128]{1,0:T(1,128)S(1)} %bitcast.4), custom_call_target="tpu_custom_call" | custom-call | tf_op jit(solution)/shard_map/infonce/pallas_call | solution.py:720
  63.6 0.7 %copy.11 = f32[128,768]{1,0:T(8,128)} copy(f32[128,768]{1,0:T(8,128)S(1)} %get-tuple-element.13) | data formatting | bytes 786432
  64.3 0.7 %copy.12 = f32[128,768]{1,0:T(8,128)} copy(f32[128,768]{1,0:T(8,128)S(1)} %get-tuple-element.14) | data formatting | bytes 786432
Async XLA Ops:
  0.6 0.7 copy-start.3
  1.3 1.0 %copy-start = (f32[128,768]{1,0:T(8,128)S(1)}, f32[128,768]{1,0:T(8,128)}, u32[]{:S(2)}) copy-start(f32[128,768]{1,0:T(8,128)} %queries_hbm.1) | copy-start | bytes 1179652
  2.3 1.0 %copy-start.1 = (f32[128,768]{1,0:T(8,128)S(1)}, f32[128,768]{1,0:T(8,128)}, u32[]{:S(2)}) copy-start(f32[128,768]{1,0:T(8,128)} %passages_hbm.1) | copy-start | bytes 1179652
  3.3 0.7 %copy-start.2 = (s32[128,32]{0,1:T(8,128)S(1)}, s32[128,32]{0,1:T(8,128)}, u32[]{:S(2)}) copy-start(s32[128,32]{0,1:T(8,128)} %param.6) | copy-start | bytes 49156

commit v5 on v4

--- a/solution.py
+++ b/solution.py
@@ -215,15 +215,21 @@
         return pbuf.at[k, pl.ds(first, size), :]
 
     def ring(at, own, to_left, to_right, to_pair, send, recv):
+        low, high = own.at[pl.ds(0, 64), :], own.at[pl.ds(64, 64), :]
         plan = [
-            (own, at(LEFT), to_right),
-            (own, at(RIGHT), to_left),
+            (low, at(LEFT, 0, 64), to_right),
+            (high, at(RIGHT, 64, 64), to_left),
             (own, at(PAIR), to_pair),
+            (high, at(LEFT, 64, 64), to_right),
+            (low, at(RIGHT, 0, 64), to_left),
             (at(LEFT, 0, 64), at(FAR, 0, 64), to_right),
             (at(RIGHT, 64, 64), at(FAR, 64, 64), to_left),
-            (at(PAIR), at(PL), to_right),
-            (at(PAIR), at(PR), to_left),
-            (at(FAR), at(PO), to_pair),
+            (at(LEFT, 0, 64), at(PL, 0, 64), to_pair),
+            (at(RIGHT, 64, 64), at(PR, 64, 64), to_pair),
+            (at(PAIR, 64, 64), at(PL, 64, 64), to_right),
+            (at(PAIR, 0, 64), at(PR, 0, 64), to_left),
+            (at(PL, 0, 64), at(PO, 0, 64), to_right),
+            (at(PR, 64, 64), at(PO, 64, 64), to_left),
         ]
         return [
             remote(src, dst, send, recv.at[k], to) for k, (src, dst, to) in enumerate(plan)
@@ -241,7 +247,7 @@
     )
     q_copies = ring(q_at, q_ref, *q_to, q_send, q_recv)
     p_copies = ring(p_at, p_ref, *p_to, p_send, p_recv)
-    for k in range(3):
+    for k in range(5):
         q_copies[k].start()
         p_copies[k].start()
 
@@ -293,18 +299,25 @@
     lax.fori_loop(1, 16, tab_start, 0)
     tabs[me_row] = table[pl.ds(pl.multiple_of((x * 4 + half * 2 + h) * 8, 8), 8), :]
 
-    for k, slot in ((0, LEFT), (1, RIGHT)):
-        q_copies[k].wait_recv()
-        q_copies[k + 3].start()
-        p_copies[k].wait_recv()
-        p_copies[k + 3].start()
-        sib_copies[slot].start()
-    q_copies[2].wait_recv()
-    q_copies[5].start()
-    q_copies[6].start()
-    p_copies[2].wait_recv()
-    p_copies[5].start()
-    p_copies[6].start()
+    def arrive(*ks):
+        for k in ks:
+            q_copies[k].wait_recv()
+            p_copies[k].wait_recv()
+
+    def forward(*ks):
+        for k in ks:
+            q_copies[k].start()
+            p_copies[k].start()
+
+    arrive(0)
+    forward(5, 7)
+    arrive(1)
+    forward(6, 8)
+    arrive(3, 4)
+    sib_copies[LEFT].start()
+    sib_copies[RIGHT].start()
+    arrive(2)
+    forward(9, 10)
     sib_copies[PAIR].start()
 
     cmax[...] = jnp.full(cmax.shape, NEG, F32)
@@ -320,20 +333,24 @@
         for n in range(slots):
             own = part[n * QB : (n + 1) * QB]
             sbuf[k + n, :, cols] = own
-            rnext[k + n] = jnp.maximum(rnext[k + n], jnp.maximum(own[:, :128], own[:, 128:]))
-
-    for k in (RIGHT, PAIR):
-        sib_copies[k].wait_recv()
-        sib_copies[k + 1].wait_recv()
-        scores(k, 2, 3)
-        scores(k, 2, 2)
-
-    for k in (3, 4):
-        q_copies[k].wait_recv()
-        p_copies[k].wait_recv()
-    q_copies[7].start()
-    p_copies[7].start()
+            top = jnp.maximum(own[:, :128], own[:, 128:])
+            rnext[c // 2, k + n] = jnp.maximum(rnext[c // 2, k + n], top)
+
+    sib_copies[ME].wait_recv()
+    sib_copies[RIGHT].wait_recv()
+    scores(RIGHT, 2, 3)
+    scores(RIGHT, 2, 2)
+
+    arrive(7)
+    forward(11)
+    arrive(8)
+    forward(12)
+    arrive(5, 6)
     sib_copies[FAR].start()
+    sib_copies[LEFT].wait_recv()
+    sib_copies[PAIR].wait_recv()
+    scores(PAIR, 2, 3)
+    scores(PAIR, 2, 2)
 
     def group(ref, send, recv):
         return remote(ref, ref, send, recv, sibling)
@@ -356,61 +373,78 @@
             mbuf[k, :, p * 128 : (p + 1) * 128] = dot_nt(rows, cols).astype(BF)
         return carry
 
-    lax.fori_loop(0, NQ, count_step, 0)
+    lax.fori_loop(FAR, NQ, count_step, 0)
     sib_copies[FAR].wait_recv()
-    scores(FAR, 1, 3)
-    scores(FAR, 1, 2)
-
-    for k, slot in ((5, PL), (6, PR), (7, PO)):
-        q_copies[k].wait_recv()
-        sib_copies[slot].start()
-        p_copies[k].wait_recv()
-
-    def levels(k):
-        csum[...] = csum[...] * jnp.exp2(cmax[...] - cnext[...])
-        cmax[...] = cnext[...]
-        top = jnp.max(rnext[k], axis=1, keepdims=True)
-        wide_ref[k] = jnp.broadcast_to(top, (QB, 128))
-
-    def sums(k, r):
+
+    def levels(half, k):
+        cols = slice(half * 512, half * 512 + 512)
+        csum[:, cols] = csum[:, cols] * jnp.exp2(cmax[:, cols] - cnext[:, cols])
+        cmax[:, cols] = cnext[:, cols]
+        top = jnp.max(rnext[half, k], axis=1, keepdims=True)
+        wide_ref[half, k] = jnp.broadcast_to(top, (QB, 128))
+
+    def sums(half, k, r):
         rows = slice(r * CH, (r + 1) * CH)
-        wide = wide_ref[k, rows, :]
+        wide = wide_ref[half, k, rows, :]
         total = jnp.zeros((CH, 128), F32)
-        for g in range(8):
+        for g in range(half * 4, half * 4 + 4):
             cols = slice(g * 128, (g + 1) * 128)
             s = sbuf[k, rows, cols]
             e = jnp.exp2(s - wide)
             total += e + e * mbuf[k, rows, cols].astype(F32)
             csum[:, cols] += jnp.exp2(eighths(s) - cmax[:, cols][None]).sum(0)
-        rsum[k, rows, :] = total
+        rsum[half, k, rows, :] = total
 
     def row_level(k):
-        top = wide_ref[k].T[0:1, :]
-        total = jnp.sum(rsum[k].T, axis=0, keepdims=True)
-        rstat[me_row, pl.ds(q_index(k), 1), :] = top + jnp.log2(total)
-
-    turn = (ME, RIGHT, LEFT, PAIR, FAR, PR, PL, PO)
-    plan = {
-        ME: [(PAIR, 2, 1), (PAIR, 2, 0)],
-        LEFT: [(PR, 2, 1), (PR, 2, 0)],
-        FAR: [(PR, 1, 3), (PR, 1, 2)],
-        PAIR: [(PO, 2, 3), (PO, 2, 2)],
-        PR: [(PO, 2, 1), (PO, 2, 0)],
-    }
+        top = jnp.maximum(wide_ref[0, k], wide_ref[1, k])
+        total = rsum[0, k] * jnp.exp2(wide_ref[0, k] - top)
+        total += rsum[1, k] * jnp.exp2(wide_ref[1, k] - top)
+        total = jnp.sum(total.T, axis=0, keepdims=True)
+        rstat[me_row, pl.ds(q_index(k), 1), :] = top.T[0:1, :] + jnp.log2(total)
+
+    def sweep(half, k, *todo):
+        levels(half, k)
+        for r in range(4):
+            sums(half, k, r)
+            for work in todo[r // 2 :: 2] if r % 2 else ():
+                scores(*work)
+
+    sweep(1, ME, (FAR, 1, 3))
+    sweep(1, RIGHT, (FAR, 1, 2))
+    sweep(1, LEFT)
+    sweep(1, PAIR)
+    sweep(1, FAR)
+    lax.fori_loop(PO, FAR, count_step, 0)
+
+    arrive(9, 10)
+    sib_copies[PL].start()
+    sib_copies[PR].start()
+    arrive(11, 12)
+    sib_copies[PO].start()
     scores(RIGHT, 2, 1)
     scores(RIGHT, 2, 0)
-    for k in turn:
-        if k == LEFT:
-            sib_copies[PR].wait_recv()
-        if k == PAIR:
-            sib_copies[PL].wait_recv()
-            sib_copies[PO].wait_recv()
-        levels(k)
-        for r in range(4):
-            sums(k, r)
-            if r % 2 and k in plan:
-                scores(*plan[k][r // 2])
-        row_level(k)
+    sweep(0, ME, (PAIR, 2, 1))
+    sweep(0, RIGHT, (PAIR, 2, 0))
+    row_level(ME)
+    row_level(RIGHT)
+    sib_copies[PR].wait_recv()
+    sweep(0, LEFT, (PR, 2, 1))
+    sweep(0, PAIR, (PR, 2, 0))
+    row_level(LEFT)
+    row_level(PAIR)
+    sib_copies[PL].wait_recv()
+    sib_copies[PO].wait_recv()
+    sweep(0, FAR, (PR, 1, 3), (PR, 1, 2))
+    row_level(FAR)
+    sweep(0, PR, (PO, 2, 3))
+    sweep(1, PR, (PO, 2, 2))
+    row_level(PR)
+    sweep(1, PL, (PO, 2, 1))
+    sweep(1, PO, (PO, 2, 0))
+    sweep(0, PL)
+    sweep(0, PO)
+    row_level(PL)
+    row_level(PO)
 
     top = jnp.max(cmax[...], axis=0, keepdims=True)
     total = jnp.sum(csum[...] * jnp.exp2(cmax[...] - top), axis=0, keepdims=True)
@@ -715,6 +749,8 @@
 
 
 def per_device(queries, passages, hard_ids, list_lengths):
+    given = (queries, passages, hard_ids.T, list_lengths.reshape(1, OWN))
+    given = [pltpu.with_memory_space_constraint(value, pltpu.HBM) for value in given]
     vm = pl.BlockSpec(memory_space=pltpu.VMEM)
     dma = pltpu.SemaphoreType.DMA
     loss, grad_queries, grad_passages = pl.pallas_call(
@@ -746,9 +782,9 @@
             pltpu.VMEM((8, COLS), F32),
             pltpu.VMEM((8, COLS), F32),
             pltpu.VMEM((8, COLS), F32),
-            pltpu.VMEM((NQ, QB, 128), F32),
-            pltpu.VMEM((NQ, QB, 128), F32),
-            pltpu.VMEM((NQ, QB, 128), F32),
+            pltpu.VMEM((2, NQ, QB, 128), F32),
+            pltpu.VMEM((2, NQ, QB, 128), F32),
+            pltpu.VMEM((2, NQ, QB, 128), F32),
             pltpu.VMEM((16, 8, QB), F32),
             pltpu.VMEM((8, 16, 128), F32),
             pltpu.VMEM((8, QB), F32),
@@ -771,9 +807,9 @@
             pltpu.VMEM((10, 1, OWN), F32),
             dma((4,)),
             dma,
-            dma((8,)),
-            dma,
-            dma((8,)),
+            dma((13,)),
+            dma,
+            dma((13,)),
             dma,
             dma((8,)),
             dma,
@@ -798,10 +834,10 @@
             dma((10,)),
         ],
         compiler_params=pltpu.CompilerParams(
-            collective_id=0, has_side_effects=True, vmem_limit_bytes=50 * 1024 * 1024
+            collective_id=0, has_side_effects=True, vmem_limit_bytes=51 * 1024 * 1024
         ),
         name="infonce",
-    )(queries, passages, hard_ids.T, list_lengths.reshape(1, OWN))
+    )(*given)
     return loss[0, 0], grad_queries, grad_passages
 
 

time: 66.4 us -> 60.8 us (0.916)
  local copies, waits for them, and re-layouts: 4.85 us -> 1.49 us
  Pallas kernels: 58.9 us -> 56.8 us
    unnamed x10 -> x2, local copies, waits for them, and re-layouts: 4.85 us -> 1.49 us
    pallas_call x1, Pallas kernels: 58.9 us -> 56.8 us  [per_device(): pl.pallas_call(kernel, out_shape=(jax.ShapeDtypeStruct((1, 1), F32), jax....]
where the time goes in v5:
time: 60.8 us; the launch traced here: 60.6 us
  Pallas kernels  56.8 us (93%)
  between operations  2.33 us (4%)
  local copies, waits for them, and re-layouts  1.49 us (2%)
    pallas_call x1, Pallas kernels, per_device(): pl.pallas_call(kernel, out_shape=(jax.ShapeDtypeStruct((1, 1), F32), jax....  56.8 us
    unnamed x2, local copies, waits for them, and re-layouts  1.49 us

profile of v5, /device:TPU:0, one launch (start us, length us, event | category | flops | bytes accessed | tf_op | source)
XLA Modules:
  0.0 60.6 jit_solution(1157104272219512267)
XLA Ops:
  0.6 56.8 %infonce.1 = (f32[1,1]{1,0:T(1,128)}, f32[128,768]{1,0:T(8,128)S(1)}, f32[128,768]{1,0:T(8,128)S(1)}) custom-call(f32[128,768]{1,0:T(8,128)} %queries_hbm.1, f32[128,768]{1,0:T(8,128)} %passages_hbm.1, s32[32,128]{1,0:T(8,128)} %bitcast.3, s32[1,128]{1,0:T(1,128)} %bitcast.4), custom_call_target="tpu_custom_call" | custom-call | tf_op jit(solution)/shard_map/infonce/pallas_call | solution.py:756
  58.0 0.7 %copy.11 = f32[128,768]{1,0:T(8,128)} copy(f32[128,768]{1,0:T(8,128)S(1)} %get-tuple-element.13) | data formatting | bytes 786432
  58.8 0.7 %copy.12 = f32[128,768]{1,0:T(8,128)} copy(f32[128,768]{1,0:T(8,128)S(1)} %get-tuple-element.14) | data formatting | bytes 786432

commit v6 on v5

--- a/solution.py
+++ b/solution.py
@@ -83,7 +83,7 @@
     dq,
     sib,
     dp,
-    most,
+    exact,
     outq,
     inq,
     outq_scale,
@@ -373,7 +373,7 @@
             mbuf[k, :, p * 128 : (p + 1) * 128] = dot_nt(rows, cols).astype(BF)
         return carry
 
-    lax.fori_loop(FAR, NQ, count_step, 0)
+    lax.fori_loop(FAR, NQ, count_step, 0, unroll=True)
     sib_copies[FAR].wait_recv()
 
     def levels(half, k):
@@ -414,7 +414,7 @@
     sweep(1, LEFT)
     sweep(1, PAIR)
     sweep(1, FAR)
-    lax.fori_loop(PO, FAR, count_step, 0)
+    lax.fori_loop(PO, FAR, count_step, 0, unroll=True)
 
     arrive(9, 10)
     sib_copies[PL].start()
@@ -523,12 +523,13 @@
 
         return part
 
-    def passage_sums(c):
+    def passage_sums(first, slots):
         def part(n):
             cols = slice(n * 256, (n + 1) * 256)
-            left = wbuf[:, :, c * 256 : (c + 1) * 256].reshape(ROWS, 256)
+            wide = slots * OWN
+            left = wbuf[:, :, first * OWN : first * OWN + wide].reshape(ROWS, wide)
             found = dot_tn(left, qbuf[...].reshape(ROWS, D)[:, cols])
-            dp[2 * c : 2 * c + 2, :, cols] = found.reshape(2, OWN, 256)
+            dp[first : first + slots, :, cols] = found.reshape(slots, OWN, 256)
 
         return part
 
@@ -539,7 +540,7 @@
 
     def query_part(k):
         def rows(first, size):
-            start = pl.multiple_of(h * OWN + first, 32)
+            start = pl.multiple_of(h * OWN + first, 16)
             return dq[k, pl.ds(start, size), :] + sib[k, first : first + size, :]
 
         return rows
@@ -548,7 +549,8 @@
         return lambda first, size: dp[p, first : first + size, :]
 
     class Sums:
-        def __init__(self, part, to, bufs, sems):
+        def __init__(self, part, to, exact, bufs, sems):
+            self.exact = exact
             to_left, to_right, to_pair = to
             self.part = part
             self.out, self.inn, self.out_scale, self.in_scale = bufs
@@ -588,48 +590,50 @@
                 for copy in self.copies(k):
                     copy.wait_recv()
 
-        def levels(self, k):
-            return jnp.broadcast_to(self.in_scale[k], (OWN, OWN)).T
-
-        def decoded(self, k, level, first, size):
+        def decoded(self, k, first, size):
             value = self.inn[k, first : first + size, :].astype(jnp.int32).astype(F32)
-            return value * jnp.concatenate([level[first : first + size]] * (D // OWN), axis=1)
+            return value * self.in_scale[k]
 
         def encode(self, k, added=()):
             block, low, high, _ = self.slots[k]
             part = self.part(block)
-            levels = {a: self.levels(a) for a in added}
-            for first in range(low, high, 32):
-                value = part(first, 32)
+            exact = self.exact
+            top = jnp.full((8, D), 1e-30, F32)
+            for first in range(low, high, 16):
+                value = part(first, 16)
                 for a in added:
-                    value = value + self.decoded(a, levels[a], first, 32)
-                top = jnp.max(jnp.abs(value), axis=1, keepdims=True)
-                top = jnp.maximum(top, 1e-30)
-                whole = jnp.round(value * (32766.0 / top)).astype(jnp.int32)
-                self.out[k, first : first + 32, :] = whole.astype(jnp.int16)
-                most[first : first + 32, :] = jnp.broadcast_to(top, (32, OWN))
-            self.out_scale[k] = most[...].T[0:1, :] * (1.0 / 32766.0)
+                    value = value + self.decoded(a, first, 16)
+                exact[first : first + 16, :] = value
+                top = jnp.maximum(top, eighths(jnp.abs(value)).max(0))
+            top = jnp.max(top, axis=0, keepdims=True)
+            scale = 32766.0 / top
+            for first in range(low, high, 16):
+                rows = slice(first, first + 16)
+                whole = jnp.round(exact[rows, :] * scale).astype(jnp.int32)
+                self.out[k, rows, :] = whole.astype(jnp.int16)
+            self.out_scale[k] = top * (1.0 / 32766.0)
 
         def finish(self, grad, positive):
             part = self.part(ME)
-            levels = {a: self.levels(a) for a in range(5, 10)}
-            for first in range(0, OWN, 32):
-                value = part(first, 32)
+            for first in range(0, OWN, 16):
+                value = part(first, 16)
                 for a in range(5, 10):
                     if self.slots[a][1] <= first < self.slots[a][2]:
-                        value = value + self.decoded(a, levels[a], first, 32)
-                rows = slice(first, first + 32)
+                        value = value + self.decoded(a, first, 16)
+                rows = slice(first, first + 16)
                 grad[rows, :] = 0.5 * (value - 2.0 * positive[rows, :].astype(F32))
 
     qs = Sums(
         query_part,
         q_to,
+        exact.at[0],
         (outq, inq, outq_scale, inq_scale),
         (gq_send, gq_recv, gq_scale_send, gq_scale_recv),
     )
     ps = Sums(
         passage_part,
         p_to,
+        exact.at[1],
         (outp, inp, outp_scale, inp_scale),
         (gp_send, gp_recv, gp_scale_send, gp_scale_recv),
     )
@@ -645,35 +649,43 @@
     def every(slots, columns):
         return [(k, c) for k in slots for c in columns]
 
-    most[...] = jnp.ones_like(most)
     rest = (FAR, PAIR, LEFT, RIGHT, ME)
     for work in every((PO, PL, PR), range(4)):
         weights(*work)
-    beside(query_sums(PO, 3), every(rest, (0, 1)))
+    beside(query_sums(PO, 3), every(rest, (0,)))
     dsib_copy(PO).start()
     dsib_copy(PL).start()
     dsib_copy(PR).start()
-    beside(passage_sums(0), every(rest, (2, 3)))
+    beside(passage_sums(PO, 2))
     dsib_copy(PO).wait_recv()
     qs.encode(0)
     ps.encode(0)
+    qs.start(0)
     ps.encode(1)
-    qs.start(0)
-    ps.start(0, 1)
+    ps.start(0)
+    for work in every(rest, (1,)):
+        weights(*work)
+    ps.start(1)
     dsib_copy(PL).wait_recv()
     qs.encode(1)
-    beside(passage_sums(1))
+    beside(passage_sums(PR, 2))
     qs.start(1)
     dsib_copy(PR).wait_recv()
     qs.encode(2)
     ps.encode(2)
     qs.start(2)
+    for work in every(rest[:2], (2, 3)):
+        weights(*work)
     ps.start(2)
     beside(query_sums(FAR, 2))
+    for work in every(rest[2:], (2, 3)):
+        weights(*work)
+    dsib_copy(FAR).start()
+    dsib_copy(PAIR).start()
     beside(query_sums(LEFT, 2))
-    for k in (FAR, PAIR, LEFT, RIGHT):
-        dsib_copy(k).start()
-    beside(passage_sums(2))
+    dsib_copy(LEFT).start()
+    dsib_copy(RIGHT).start()
+    beside(passage_sums(PAIR, 3))
     dsib_copy(FAR).wait_recv()
     qs.arrive(0)
     qs.encode(3, [0])
@@ -683,26 +695,26 @@
     ps.encode(3, [0])
     ps.encode(4, [0])
     ps.start(3, 4)
+    ps.encode(6)
+    ps.encode(7)
     dsib_copy(LEFT).wait_recv()
     qs.encode(6)
     dsib_copy(RIGHT).wait_recv()
     qs.encode(7)
-    beside(passage_sums(3))
-    qs.start(6, 7)
+    ps.start(6, 7)
     dsib_copy(PAIR).wait_recv()
     qs.arrive(1, 2)
     qs.encode(5, [1, 2])
-    ps.encode(6)
-    ps.encode(7)
-    qs.start(5)
+    qs.start(6, 7)
     ps.arrive(1, 2)
     ps.encode(5, [1, 2])
-    ps.start(6, 7)
+    qs.start(5)
+    ps.start(5)
     beside(query_sums(ME, 1))
-    ps.start(5)
-    dsib_copy(ME).start()
     lax.fori_loop(1, 8, lr_start, 0)
     lax.fori_loop(1, 16, lc_start, 0)
+    dsib_copy(ME).start()
+    beside(passage_sums(ME, 1))
     qs.arrive(3)
     qs.encode(8, [3])
     qs.arrive(4)
@@ -796,15 +808,15 @@
             pltpu.VMEM((NQ, QB, D), F32),
             pltpu.VMEM((NQ, OWN, D), F32),
             pltpu.VMEM((NP, OWN, D), F32),
-            pltpu.VMEM((OWN, OWN), F32),
+            pltpu.VMEM((2, OWN, D), F32),
             pltpu.VMEM((10, OWN, D), jnp.int16),
             pltpu.VMEM((10, OWN, D), jnp.int16),
-            pltpu.VMEM((10, 1, OWN), F32),
-            pltpu.VMEM((10, 1, OWN), F32),
+            pltpu.VMEM((10, 1, D), F32),
+            pltpu.VMEM((10, 1, D), F32),
             pltpu.VMEM((10, OWN, D), jnp.int16),
             pltpu.VMEM((10, OWN, D), jnp.int16),
-            pltpu.VMEM((10, 1, OWN), F32),
-            pltpu.VMEM((10, 1, OWN), F32),
+            pltpu.VMEM((10, 1, D), F32),
+            pltpu.VMEM((10, 1, D), F32),
             dma((4,)),
             dma,
             dma((13,)),

time: 60.8 us -> 60.3 us (level)
  Pallas kernels: 56.8 us -> 56 us
    pallas_call x1, Pallas kernels: 56.8 us -> 56 us  [per_device(): pl.pallas_call(kernel, out_shape=(jax.ShapeDtypeStruct((1, 1), F32), jax....]
where the time goes in v6:
time: 60.3 us; the launch traced here: 59.8 us
  Pallas kernels  56 us (93%)
  between operations  2.33 us (4%)
  local copies, waits for them, and re-layouts  1.49 us (2%)
    pallas_call x1, Pallas kernels, per_device(): pl.pallas_call(kernel, out_shape=(jax.ShapeDtypeStruct((1, 1), F32), jax....  56 us
    unnamed x2, local copies, waits for them, and re-layouts  1.49 us

profile of v6, /device:TPU:0, one launch (start us, length us, event | category | flops | bytes accessed | tf_op | source)
XLA Modules:
  0.0 59.8 jit_solution(4721537061661066900)
XLA Ops:
  0.6 56.0 %infonce.1 = (f32[1,1]{1,0:T(1,128)}, f32[128,768]{1,0:T(8,128)S(1)}, f32[128,768]{1,0:T(8,128)S(1)}) custom-call(f32[128,768]{1,0:T(8,128)} %queries_hbm.1, f32[128,768]{1,0:T(8,128)} %passages_hbm.1, s32[32,128]{1,0:T(8,128)} %bitcast.3, s32[1,128]{1,0:T(1,128)} %bitcast.4), custom_call_target="tpu_custom_call" | custom-call | tf_op jit(solution)/shard_map/infonce/pallas_call | solution.py:768
  57.2 0.7 %copy.11 = f32[128,768]{1,0:T(8,128)} copy(f32[128,768]{1,0:T(8,128)S(1)} %get-tuple-element.13) | data formatting | bytes 786432
  57.9 0.7 %copy.12 = f32[128,768]{1,0:T(8,128)} copy(f32[128,768]{1,0:T(8,128)S(1)} %get-tuple-element.14) | data formatting | bytes 786432

commit v7 on v6

--- a/solution.py
+++ b/solution.py
@@ -685,7 +685,8 @@
     beside(query_sums(LEFT, 2))
     dsib_copy(LEFT).start()
     dsib_copy(RIGHT).start()
-    beside(passage_sums(PAIR, 3))
+    lax.fori_loop(1, 8, lr_start, 0)
+    lax.fori_loop(1, 16, lc_start, 0)
     dsib_copy(FAR).wait_recv()
     qs.arrive(0)
     qs.encode(3, [0])
@@ -695,24 +696,23 @@
     ps.encode(3, [0])
     ps.encode(4, [0])
     ps.start(3, 4)
+    beside(passage_sums(PAIR, 3))
+    dsib_copy(PAIR).wait_recv()
+    qs.arrive(1, 2)
+    qs.encode(5, [1, 2])
+    ps.arrive(1, 2)
+    ps.encode(5, [1, 2])
+    qs.start(5)
     ps.encode(6)
     ps.encode(7)
+    ps.start(5)
     dsib_copy(LEFT).wait_recv()
     qs.encode(6)
     dsib_copy(RIGHT).wait_recv()
     qs.encode(7)
     ps.start(6, 7)
-    dsib_copy(PAIR).wait_recv()
-    qs.arrive(1, 2)
-    qs.encode(5, [1, 2])
     qs.start(6, 7)
-    ps.arrive(1, 2)
-    ps.encode(5, [1, 2])
-    qs.start(5)
-    ps.start(5)
     beside(query_sums(ME, 1))
-    lax.fori_loop(1, 8, lr_start, 0)
-    lax.fori_loop(1, 16, lc_start, 0)
     dsib_copy(ME).start()
     beside(passage_sums(ME, 1))
     qs.arrive(3)

time: 60.3 us -> 59.9 us (level)
  no operation moved by 1% of the time
where the time goes in v7:
time: 59.9 us; the launch traced here: 59.4 us
  Pallas kernels  55.5 us (93%)
  between operations  2.33 us (4%)
  local copies, waits for them, and re-layouts  1.49 us (2%)
    pallas_call x1, Pallas kernels, per_device(): pl.pallas_call(kernel, out_shape=(jax.ShapeDtypeStruct((1, 1), F32), jax....  55.5 us
    unnamed x2, local copies, waits for them, and re-layouts  1.49 us

profile of v7, /device:TPU:0, one launch (start us, length us, event | category | flops | bytes accessed | tf_op | source)
XLA Modules:
  0.0 59.4 jit_solution(17263269251253110546)
XLA Ops:
  0.6 55.5 %infonce.1 = (f32[1,1]{1,0:T(1,128)}, f32[128,768]{1,0:T(8,128)S(1)}, f32[128,768]{1,0:T(8,128)S(1)}) custom-call(f32[128,768]{1,0:T(8,128)} %queries_hbm.1, f32[128,768]{1,0:T(8,128)} %passages_hbm.1, s32[32,128]{1,0:T(8,128)} %bitcast.3, s32[1,128]{1,0:T(1,128)} %bitcast.4), custom_call_target="tpu_custom_call" | custom-call | tf_op jit(solution)/shard_map/infonce/pallas_call | solution.py:768
  56.7 0.7 %copy.11 = f32[128,768]{1,0:T(8,128)} copy(f32[128,768]{1,0:T(8,128)S(1)} %get-tuple-element.13) | data formatting | bytes 786432
  57.5 0.7 %copy.12 = f32[128,768]{1,0:T(8,128)} copy(f32[128,768]{1,0:T(8,128)S(1)} %get-tuple-element.14) | data formatting | bytes 786432

commit v8 on v7

--- a/solution.py
+++ b/solution.py
@@ -685,8 +685,6 @@
     beside(query_sums(LEFT, 2))
     dsib_copy(LEFT).start()
     dsib_copy(RIGHT).start()
-    lax.fori_loop(1, 8, lr_start, 0)
-    lax.fori_loop(1, 16, lc_start, 0)
     dsib_copy(FAR).wait_recv()
     qs.arrive(0)
     qs.encode(3, [0])
@@ -712,6 +710,8 @@
     qs.encode(7)
     ps.start(6, 7)
     qs.start(6, 7)
+    lax.fori_loop(1, 8, lr_start, 0)
+    lax.fori_loop(1, 16, lc_start, 0)
     beside(query_sums(ME, 1))
     dsib_copy(ME).start()
     beside(passage_sums(ME, 1))

time: 59.9 us -> 60.6 us (1.012)
    pallas_call x1, Pallas kernels: 55.5 us -> 56.1 us  [per_device(): pl.pallas_call(kernel, out_shape=(jax.ShapeDtypeStruct((1, 1), F32), jax....]
where the time goes in v8:
time: 60.6 us; the launch traced here: 60 us
  Pallas kernels  56.1 us (93%)
  between operations  2.33 us (4%)
  local copies, waits for them, and re-layouts  1.49 us (2%)
    pallas_call x1, Pallas kernels, per_device(): pl.pallas_call(kernel, out_shape=(jax.ShapeDtypeStruct((1, 1), F32), jax....  56.1 us
    unnamed x2, local copies, waits for them, and re-layouts  1.49 us

profile of v8, /device:TPU:0, one launch (start us, length us, event | category | flops | bytes accessed | tf_op | source)
XLA Modules:
  0.0 60.0 jit_solution(440729852377124415)
XLA Ops:
  0.6 56.1 %infonce.1 = (f32[1,1]{1,0:T(1,128)}, f32[128,768]{1,0:T(8,128)S(1)}, f32[128,768]{1,0:T(8,128)S(1)}) custom-call(f32[128,768]{1,0:T(8,128)} %queries_hbm.1, f32[128,768]{1,0:T(8,128)} %passages_hbm.1, s32[32,128]{1,0:T(8,128)} %bitcast.3, s32[1,128]{1,0:T(1,128)} %bitcast.4), custom_call_target="tpu_custom_call" | custom-call | tf_op jit(solution)/shard_map/infonce/pallas_call | solution.py:768
  57.3 0.7 %copy.11 = f32[128,768]{1,0:T(8,128)} copy(f32[128,768]{1,0:T(8,128)S(1)} %get-tuple-element.13) | data formatting | bytes 786432
  58.1 0.7 %copy.12 = f32[128,768]{1,0:T(8,128)} copy(f32[128,768]{1,0:T(8,128)S(1)} %get-tuple-element.14) | data formatting | bytes 786432
